TPU v7x, 32 devices: a whole 2x2x4 slice. The times are simulated.
32 devices in a mesh: seq: 8 (over y, x, core), mp: 4 (over z).
Axes of the slice: x: 2, y: 2, z: 4, core: 2. Of those that a mesh axis runs over, the one named last changes fastest.
Arguments:
- tokens: bfloat16 [64, 2048, 1024], P('mp', 'seq'), may hold values from -6 to 6
- cotangent: bfloat16 [64, 2048, 1024], P('mp', 'seq'), may hold values from -6 to 6
- lengths: int32 [64], P('mp'), may hold values from 256 to 2048, as said below
- routed: int32 [64, 256], P('mp', 'seq'), may hold values from 0 to 2047, as said below
- gain_attn: float32 [1024], replicated, may hold values from 0.5 to 1.5
- gain_mlp: float32 [1024], replicated, may hold values from 0.5 to 1.5
- router: float32 [1024], replicated, may hold values from -0.1875 to 0.1875
- w_qkv: bfloat16 [3, 1024, 1024], P(None, None, 'mp'), may hold values from -0.1875 to 0.1875
- w_out: bfloat16 [1024, 1024], P('mp'), may hold values from -1.5 to 1.5
- w_mlp: bfloat16 [4096, 2, 1024], P('mp'), may hold values from -0.1875 to 0.1875
Outputs:
- layer_out: bfloat16 [64, 2048, 1024], P('mp', 'seq')
- grad_tokens: bfloat16 [64, 2048, 1024], P('mp', 'seq')
- grad_gain_attn: float32 [1024], replicated
- grad_gain_mlp: float32 [1024], replicated
- grad_router: float32 [1024], replicated
- grad_qkv: float32 [3, 1024, 1024], P(None, None, 'mp')
- grad_out: float32 [1024, 1024], P('mp')
- grad_mlp: float32 [4096, 2, 1024], P('mp')
Inputs may be any that keep to these rules, and one draw needn't show every extreme that they name: `lengths`: multiples of 8; of the two sequences 2 i and 2 i + 1 (aligned pairs) at most one is longer than 1024; among the 16 sequences of each index of mp one has length 2048 and its partner in the pair has length 256. `routed`: entry j of a sequence lies in 8 j to 8 j + 7; entries with j at or past lengths / 8 point at padding.
All inputs are finite; a program needn't handle non-finite values.
Results may differ from a plain program's by a relative error of at most 0.017.
Values may be sent and summed in bfloat16 or wider, within the bound.
No kernel may reach another device: no remote copies, remote signals or barrier semaphores. Data moves between devices by JAX's collectives and lax.ppermute only.
A program may use at most 192 MiB of HBM per device.

v0:
```python
import jax
import jax.numpy as jnp
from jax import lax
from jax.sharding import PartitionSpec as P

HEAD = 64


EPSILON = 1e-06
NEGATIVE = -1e30
BEST = lax.Precision.HIGHEST
CONTRACT_ROWS = (((0,), (0,)), ((), ()))
CONTRACT_COLS = (((1,), (1,)), ((), ()))


def rms_scale(values):
    return lax.rsqrt(jnp.mean(values * values, axis=-1, keepdims=True) + EPSILON)


def norm_back(grad_normed, unit_rows, scale, gain):
    scaled = gain * grad_normed
    return scale * (scaled - unit_rows * jnp.mean(unit_rows * scaled, axis=-1, keepdims=True))


def gelu_tanh(values):
    return jax.nn.gelu(values, approximate=True)


def split_heads(heads_in, unit_rows):
    local_width = heads_in.shape[2]
    batches = heads_in.shape[1] // unit_rows
    shaped = heads_in.reshape(3, batches, unit_rows, local_width // HEAD, HEAD)
    return (shaped[0], shaped[1], shaped[2])


def masked_scores(query, keys, split_row):
    raw = jnp.einsum("sqhd,skhd->shqk", query, keys, preferred_element_type=jnp.float32) * HEAD ** (
        -0.5
    )
    row_pos = lax.broadcasted_iota(jnp.int32, raw.shape, 2)
    col_pos = lax.broadcasted_iota(jnp.int32, raw.shape, 3)
    same = (row_pos >= split_row) == (col_pos >= split_row)
    return jnp.where(same & (row_pos >= col_pos), raw, NEGATIVE)


def holder_pass(held_rows, gain_attn, gain_mlp, router, w_qkv, w_out, w_mlp, unit_rows, split_row):
    held_float = held_rows.astype(jnp.float32)
    scale_one = rms_scale(held_float)
    unit_one = held_float * scale_one
    normed_one = (unit_one * gain_attn).astype(jnp.bfloat16)
    gate = jax.nn.sigmoid(jnp.dot(held_float, router, precision=BEST))
    normed_all = lax.all_gather(normed_one, "mp", axis=0, tiled=True)
    heads_in = jnp.einsum(
        "rd,cde->cre", normed_all, w_qkv, preferred_element_type=jnp.float32
    ).astype(jnp.bfloat16)
    query, keys, values = split_heads(heads_in, unit_rows)
    scores = masked_scores(query, keys, split_row)
    peak = jnp.max(scores, axis=-1, keepdims=True)
    raised = jnp.exp(scores - peak)
    totals = jnp.sum(raised, axis=-1, keepdims=True)
    weights = (raised / totals).astype(jnp.bfloat16)
    log_total = peak + jnp.log(totals)
    mixed = jnp.einsum(
        "shqk,skhd->sqhd", weights, values, preferred_element_type=jnp.float32
    ).astype(jnp.bfloat16)
    mixed = mixed.reshape(normed_all.shape[0], heads_in.shape[2])
    attended = lax.psum_scatter(
        jnp.dot(mixed, w_out, preferred_element_type=jnp.float32),
        "mp",
        scatter_dimension=0,
        tiled=True,
    )
    middle = held_float + attended
    scale_two = rms_scale(middle)
    unit_two = middle * scale_two
    normed_two = (unit_two * gain_mlp).astype(jnp.bfloat16)
    normed_mid = lax.all_gather(normed_two, "mp", axis=0, tiled=True)
    upward = lax.dot_general(
        normed_mid, w_mlp[:, 0, :], CONTRACT_COLS, preferred_element_type=jnp.float32
    )
    active = gelu_tanh(upward).astype(jnp.bfloat16)
    feed = lax.psum_scatter(
        jnp.dot(active, w_mlp[:, 1, :], preferred_element_type=jnp.float32).astype(jnp.bfloat16),
        "mp",
        scatter_dimension=0,
        tiled=True,
    ).astype(jnp.float32)
    return (
        held_float,
        scale_one,
        unit_one,
        gate,
        normed_all,
        heads_in,
        log_total,
        mixed,
        attended,
        scale_two,
        unit_two,
        normed_mid,
        upward,
        active,
        attended + feed,
        w_mlp,
    )


def on_device(tokens, cotangent, lengths, routed, gain_attn, gain_mlp, router, w_qkv, w_out, w_mlp):
    group, span, width = tokens.shape
    slots = routed.shape[1]
    ranks = lax.axis_size("seq")
    held = group // ranks
    seq_rows = slots * ranks
    rows = held * seq_rows
    inner = routed % 8
    place = lax.axis_index("seq") * slots + lax.broadcasted_iota(jnp.int32, routed.shape, 1)
    live = place < (lengths // 8)[:, None]
    token_grid = tokens.reshape(group, slots, 8, width)
    grad_grid = cotangent.reshape(group, slots, 8, width)
    pick = lax.broadcasted_iota(jnp.int32, (group, slots, 8), 2) == inner[:, :, None]
    chosen = jnp.take_along_axis(token_grid, inner[:, :, None, None], axis=2)
    chosen_grad = jnp.take_along_axis(grad_grid, inner[:, :, None, None], axis=2)
    chosen_grad = jnp.where(live[:, :, None, None], chosen_grad, jnp.zeros_like(chosen_grad))
    got_tokens, got_grads = (
        lax.all_to_all(
            chosen.reshape(ranks, held, 1, slots, width),
            "seq",
            split_axis=0,
            concat_axis=2,
            tiled=True,
        ),
        lax.all_to_all(
            chosen_grad.reshape(ranks, held, 1, slots, width),
            "seq",
            split_axis=0,
            concat_axis=2,
            tiled=True,
        ),
    )
    held_rows = got_tokens.reshape(rows, width)
    held_grads = got_grads.reshape(rows, width)
    first_pass = holder_pass(
        held_rows, gain_attn, gain_mlp, router, w_qkv, w_out, w_mlp, seq_rows, seq_rows
    )
    returned = (first_pass[3][:, None] * first_pass[14]).astype(jnp.bfloat16)
    saved = holder_pass(
        held_rows, gain_attn, gain_mlp, router, w_qkv, w_out, w_mlp, seq_rows, seq_rows
    )
    (
        held_float,
        scale_one,
        unit_one,
        gate,
        normed_all,
        heads_in,
        log_total,
        mixed,
        attended,
        scale_two,
        unit_two,
        normed_mid,
        upward,
        active,
        delta,
        full_mlp,
    ) = saved
    grad_rows = held_grads.astype(jnp.float32)
    grad_logit = jnp.sum(grad_rows * delta, axis=-1) * gate * (1.0 - gate)
    router_part = jnp.dot(grad_logit, held_float, precision=BEST)
    grad_feed = (gate[:, None] * grad_rows).astype(jnp.bfloat16)
    feed_all = lax.all_gather(grad_feed, "mp", axis=0, tiled=True)
    grad_active = lax.dot_general(
        feed_all, w_mlp[:, 1, :], CONTRACT_COLS, preferred_element_type=jnp.float32
    )
    unused, gelu_pull = jax.vjp(gelu_tanh, upward)
    grad_upward = gelu_pull(grad_active)[0].astype(jnp.bfloat16)
    up_part = lax.dot_general(
        grad_upward, normed_mid, CONTRACT_ROWS, preferred_element_type=jnp.float32
    )
    down_part = lax.dot_general(active, feed_all, CONTRACT_ROWS, preferred_element_type=jnp.float32)
    mlp_local = jnp.stack([up_part, down_part], axis=1)
    grad_normed_two = lax.psum_scatter(
        jnp.dot(grad_upward, w_mlp[:, 0, :], preferred_element_type=jnp.float32),
        "mp",
        scatter_dimension=0,
        tiled=True,
    )
    grad_middle = norm_back(grad_normed_two, unit_two, scale_two, gain_mlp)
    mlp_gain_part = jnp.sum(grad_normed_two * unit_two, axis=0)
    grad_attended = (gate[:, None] * grad_rows + grad_middle).astype(jnp.bfloat16)
    attended_all = lax.all_gather(grad_attended, "mp", axis=0, tiled=True)
    out_local = lax.dot_general(
        mixed, attended_all, CONTRACT_ROWS, preferred_element_type=jnp.float32
    )
    grad_mixed = lax.dot_general(
        attended_all, w_out, CONTRACT_COLS, preferred_element_type=jnp.float32
    ).astype(jnp.bfloat16)
    query, keys, values = split_heads(heads_in, seq_rows)
    grad_heads_mixed = grad_mixed.reshape(query.shape)
    scores = masked_scores(query, keys, seq_rows)
    shares = jnp.exp(scores - log_total)
    weights = shares.astype(jnp.bfloat16)
    grad_weights = jnp.einsum(
        "sqhd,skhd->shqk", grad_heads_mixed, values, preferred_element_type=jnp.float32
    )
    grad_scores = (
        shares * (grad_weights - jnp.sum(shares * grad_weights, axis=-1, keepdims=True))
    ).astype(jnp.bfloat16)
    grad_query = jnp.einsum(
        "shqk,skhd->sqhd", grad_scores, keys, preferred_element_type=jnp.float32
    ) * HEAD ** (-0.5)
    grad_keys = jnp.einsum(
        "shqk,sqhd->skhd", grad_scores, query, preferred_element_type=jnp.float32
    ) * HEAD ** (-0.5)
    grad_values = jnp.einsum(
        "shqk,sqhd->skhd", weights, grad_heads_mixed, preferred_element_type=jnp.float32
    )
    grad_heads = (
        jnp.stack([grad_query, grad_keys, grad_values]).astype(jnp.bfloat16).reshape(heads_in.shape)
    )
    qkv_local = jnp.einsum(
        "rd,cre->cde", normed_all, grad_heads, preferred_element_type=jnp.float32
    )
    grad_normed_one = lax.psum_scatter(
        jnp.einsum("cre,cde->rd", grad_heads, w_qkv, preferred_element_type=jnp.float32).astype(
            jnp.bfloat16
        ),
        "mp",
        scatter_dimension=0,
        tiled=True,
    ).astype(jnp.float32)
    attn_gain_part = jnp.sum(grad_normed_one * unit_one, axis=0)
    grad_picked = (
        grad_middle
        + norm_back(grad_normed_one, unit_one, scale_one, gain_attn)
        + grad_logit[:, None] * router
    ).astype(jnp.bfloat16)
    back_out, back_grad = (
        lax.all_to_all(
            returned.reshape(1, held, ranks, slots, width),
            "seq",
            split_axis=2,
            concat_axis=0,
            tiled=True,
        ),
        lax.all_to_all(
            grad_picked.reshape(1, held, ranks, slots, width),
            "seq",
            split_axis=2,
            concat_axis=0,
            tiled=True,
        ),
    )
    keep = pick[:, :, :, None] & live[:, :, None, None]
    back_out = back_out.reshape(group, slots, 1, width).astype(jnp.float32)
    back_grad = back_grad.reshape(group, slots, 1, width).astype(jnp.float32)
    layer_out = (token_grid.astype(jnp.float32) + jnp.where(keep, back_out, 0.0)).astype(
        jnp.bfloat16
    )
    grad_tokens = (grad_grid.astype(jnp.float32) + jnp.where(keep, back_grad, 0.0)).astype(
        jnp.bfloat16
    )
    grad_qkv, grad_out, grad_mlp = (
        lax.psum(qkv_local.astype(jnp.bfloat16), "seq").astype(jnp.float32),
        lax.psum(out_local.astype(jnp.bfloat16), "seq").astype(jnp.float32),
        lax.psum(mlp_local.astype(jnp.bfloat16), "seq").astype(jnp.float32),
    )
    grad_gain_attn, grad_gain_mlp, grad_router = lax.psum(
        (attn_gain_part, mlp_gain_part, router_part), ("seq", "mp")
    )
    return (
        layer_out.reshape(group, span, width),
        grad_tokens.reshape(group, span, width),
        grad_gain_attn,
        grad_gain_mlp,
        grad_router,
        grad_qkv,
        grad_out,
        grad_mlp,
    )


def solution(mesh):
    placed = (
        P("mp", "seq", None),
        P("mp", "seq", None),
        P("mp"),
        P("mp", "seq"),
        P(),
        P(),
        P(),
        P(None, None, "mp"),
        P("mp", None),
        P("mp", None, None),
    )
    return jax.shard_map(
        on_device,
        mesh=mesh,
        in_specs=placed,
        out_specs=(
            P("mp", "seq", None),
            P("mp", "seq", None),
            P(),
            P(),
            P(),
            P(None, None, "mp"),
            P("mp", None),
            P("mp", None, None),
        ),
        check_vma=False,
    )
```

profile of v0, /device:TPU:0, one launch (start us, length us, event | category | flops | bytes accessed | tf_op | source)
XLA Modules:
  0.0 1143.7 jit_solution(17167783072121866484)
XLA Ops:
  9.4 8.4 gather_fusion.1
  17.9 8.4 gather_fusion
  29.2 20.3 %all_to_all.42 = bf16[8,2,1,32,1024]{4,3,1,2,0:T(8,128)(2,1)S(1)} all-to-all(bf16[8,2,1,32,1024]{4,3,1,2,0:T(8,128)(2,1)S(1)} %bitcast.192), channel_id=1, replica_groups=mesh['seq'=8,'mp'=4] {'seq'}, dimensions={0} | all-to-all | bytes 2097152 | tf_op jit(solution)/shard_map/all_to_all | solution.py:125
  53.2 80.2 %all-gather.5.cloned.1.call-done = bf16[2048,1024]{1,0:T(8,128)(2,1)} async-done(((bf16[512,1024]{1,0:T(8,128)(2,1)}), bf16[2048,1024]{1,0:T(8,128)(2,1)}) %all-gather.5.cloned.1.call-update) | async-done | bytes 4194320 | tf_op jit(solution)/shard_map/all_gather | solution.py:52
  133.4 5.6 fusion.25
  140.8 4.6 reshape.258
  176.9 4.7 fusion.73
  181.7 143.1 %reduce-scatter.5.cloned.1.call-done = f32[512,1024]{1,0:T(8,128)} async-done(((f32[2048,1024]{1,0:T(8,128)}), f32[512,1024]{1,0:T(8,128)}) %reduce-scatter.5.cloned.1.call-update) | async-done | bytes 2097168 | tf_op jit(solution)/shard_map/reduce_scatter | solution.py:67
  328.4 19.4 %all_to_all.43 = bf16[8,2,1,32,1024]{4,3,1,2,0:T(8,128)(2,1)S(1)} all-to-all(bf16[8,2,1,32,1024]{4,3,1,2,0:T(8,128)(2,1)} %bitcast.191), channel_id=1, replica_groups=mesh['seq'=8,'mp'=4] {'seq'}, dimensions={0} | all-to-all | bytes 2097152 | tf_op jit(solution)/shard_map/all_to_all | solution.py:132
  350.9 10.2 fusion.69
  361.1 48.9 %all-gather.7.cloned.1.call-done = bf16[2048,1024]{1,0:T(8,128)(2,1)} async-done(((bf16[512,1024]{1,0:T(8,128)(2,1)}), bf16[2048,1024]{1,0:T(8,128)(2,1)}) %all-gather.7.cloned.1.call-update) | async-done | bytes 4194320 | tf_op jit(solution)/shard_map/all_gather | solution.py:77
  410.0 10.3 fusion.58
  423.7 7.2 convolution_convert_fusion
  431.0 60.3 %all-gather.9.cloned.1.call-done = bf16[2048,1024]{1,0:T(8,128)(2,1)} async-done(((bf16[512,1024]{1,0:T(8,128)(2,1)}), bf16[2048,1024]{1,0:T(8,128)(2,1)}) %all-gather.9.cloned.1.call-update) | async-done | bytes 4194320 | tf_op jit(solution)/shard_map/all_gather | solution.py:171
  491.3 14.3 %fusion.10 = bf16[2048,1024]{1,0:T(8,128)(2,1)S(1)} fusion(f32[2048,1024]{1,0:T(8,128)} %copy-done.36, bf16[2048,1024]{1,0:T(8,128)(2,1)} %all-gather.9.cloned.1.call-done, bf16[1024,1,1024]{2,1,0:T(2,128)(2,1)} %get-tuple-element.63), kind=kOutput, calls=%fused_computation.16 | convolution fusion | flops 4336910336 | bytes 18874368 | tf_op jit(solution)/shard_map/dot_general | solution.py:172
  507.6 6.9 fusion.57
  514.6 54.3 %reduce-scatter.7.cloned.1.call-done = bf16[512,1024]{1,0:T(8,128)(2,1)} async-done(((bf16[2048,1024]{1,0:T(8,128)(2,1)}), bf16[512,1024]{1,0:T(8,128)(2,1)}) %reduce-scatter.7.cloned.1.call-update) | async-done | bytes 1048592 | tf_op jit(solution)/shard_map/reduce_scatter | solution.py:82
  568.9 147.9 %reduce-scatter.9.cloned.1.call-done = f32[512,1024]{1,0:T(8,128)} async-done(((f32[2048,1024]{1,0:T(8,128)}), f32[512,1024]{1,0:T(8,128)}) %reduce-scatter.9.cloned.1.call-update) | async-done | bytes 2097168 | tf_op jit(solution)/shard_map/reduce_scatter | solution.py:182
  716.8 5.3 multiply_reduce_fusion.1
  724.0 81.6 %all-gather.11.cloned.1.call-done = bf16[2048,1024]{1,0:T(8,128)(2,1)} async-done(((bf16[512,1024]{1,0:T(8,128)(2,1)}), bf16[2048,1024]{1,0:T(8,128)(2,1)}) %all-gather.11.cloned.1.call-update) | async-done | bytes 4194320 | tf_op jit(solution)/shard_map/all_gather | solution.py:191
  810.0 4.8 reshape.259
  818.8 6.3 fusion.52
  825.0 5.6 multiply_reduce_fusion
  866.3 5.1 bitcast_convert_fusion
  871.6 8.2 convert_bitcast_fusion.2
  879.8 9.0 convert_bitcast_fusion.1
  896.2 4.5 fusion.44
  907.5 39.3 %reduce-scatter.11.cloned.1.call-done = bf16[512,1024]{1,0:T(8,128)(2,1)} async-done(((bf16[2048,1024]{1,0:T(8,128)(2,1)}), bf16[512,1024]{1,0:T(8,128)(2,1)}) %reduce-scatter.11.cloned.1.call-update) | async-done | bytes 1048592 | tf_op jit(solution)/shard_map/reduce_scatter | solution.py:224
  961.3 106.0 %all-reduce.4.cloned.1.call-done = (bf16[3,1024,256]{1,2,0:T(8,128)(2,1)}, bf16[1024,2,1024]{2,0,1:T(8,128)(2,1)}, bf16[256,1024]{1,0:T(8,128)(2,1)}) async-done(((bf16[3,1024,256]{1,2,0:T(8,128)(2,1)}, bf16[1024,2,1024]{2,0,1:T(8,128)(2,1)}, bf16[256,1024]{1,0:T(8,128)(2,1)}), (bf16[3,1024,256]{1,2,0:T(8,128)(2,1)}, bf16[1024,2,1024]{2,0,1:T(8,128)(2,1)}, ...) | async-done | bytes 6291472 | tf_op jit(solution)/shard_map/psum | solution.py:264
  1072.5 9.9 copy.186
  1082.4 39.6 %all-reduce = (f32[1024]{0:T(1024)}, f32[1024]{0:T(1024)}, f32[1024]{0:T(1024)}) all-reduce(f32[1024]{0:T(1024)S(1)} %get-tuple-element.51, f32[1024]{0:T(1024)S(1)} %get-tuple-element.49, f32[1024]{0:T(1024)S(1)} %bitcast.204), channel_id=1, replica_groups=mesh['seq'=8,'mp'=4] {'seq','mp'}, use_global_device_ids=true, to_apply=%region_13.15 | all-reduce | flops 3072 | bytes 24576 | tf_op jit(solution)/shard_map/psum | solution.py:268
  1123.9 13.1 %fusion.1 = (bf16[16,256,1024]{2,1,0:T(8,128)(2,1)}, bf16[16,256,1024]{2,1,0:T(8,128)(2,1)}) fusion(bf16[16,256,1024]{2,1,0:T(8,128)(2,1)} %param.13, f32[16,32,1024]{2,1,0:T(8,128)S(1)} %bitcast.185, pred[16,256]{1,0:T(8,128)(4,1)S(1)} %copy.149, f32[16,32,1024]{2,1,0:T(8,128)S(1)} %bitcast.184, bf16[16,256,1024]{2,1,0:T(8,128)(2,1)} %param.12), kind=kLoop, calls=%fused_computation.4 | loop fusion | flops 33554432 | bytes 37752832 | tf_op jit(solution)/shard_map/convert_element_type | solution.py:260
  (173 shorter events, 135.8 us)
Async XLA Ops:
  7.2 126.3 %copy-start = (bf16[3,1024,256]{2,1,0:T(8,128)(2,1)S(1)}, bf16[3,1024,256]{2,1,0:T(8,128)(2,1)}, u32[]{:S(2)}) copy-start(bf16[3,1024,256]{2,1,0:T(8,128)(2,1)} %param.19) | copy-start | bytes 4718596
  7.2 126.2 %all-gather.5.cloned.1.call-start = ((), (), s32[]{:S(2)}) async-start(), calls=%async_computation.8 | async-start | bytes 5242880 | tf_op jit(solution)/shard_map/all_gather | solution.py:52
  26.4 25.4 %copy-start.25 = (f32[1024]{0:T(1024)S(1)}, f32[1024]{0:T(1024)}, u32[]{:S(2)}) copy-start(f32[1024]{0:T(1024)} %param.16) | copy-start | bytes 12292
  50.5 88.6 %copy-start.27 = (f32[512]{0:T(512)}, f32[512]{0:T(512)S(1)}, u32[]{:S(2)}) copy-start(f32[512]{0:T(512)S(1)} %rsqrt.22) | copy-start | bytes 6148
  53.1 271.6 %reduce-scatter.5.cloned.1.call-start = ((), (), s32[]{:S(2)}) async-start(), calls=%async_computation.9 | async-start | bytes 10485760 | tf_op jit(solution)/shard_map/reduce_scatter | solution.py:67
  170.0 3.4 copy-start.1
  181.6 145.3 %copy-start.24 = (f32[1024]{0:T(1024)S(1)}, f32[1024]{0:T(1024)}, u32[]{:S(2)}) copy-start(f32[1024]{0:T(1024)} %param.17) | copy-start | bytes 12292
  181.6 228.4 %all-gather.7.cloned.1.call-start = ((), (), s32[]{:S(2)}) async-start(), calls=%async_computation.10 | async-start | bytes 5242880 | tf_op jit(solution)/shard_map/all_gather | solution.py:77
  328.4 163.0 %all-gather.9.cloned.1.call-start = ((), (), s32[]{:S(2)}) async-start(), calls=%async_computation.12 | async-start | bytes 5242880 | tf_op jit(solution)/shard_map/all_gather | solution.py:171
  350.9 218.0 %reduce-scatter.7.cloned.1.call-start = ((), (), s32[]{:S(2)}) async-start(), calls=%async_computation.11 | async-start | bytes 5242880 | tf_op jit(solution)/shard_map/reduce_scatter | solution.py:82
  410.0 13.7 %copy-start.18 = (bf16[1024,1,1024]{2,1,0:T(2,128)(2,1)S(1)}, bf16[1024,1,1024]{2,1,0:T(2,128)(2,1)}, u32[]{:S(2)}) copy-start(bf16[1024,1,1024]{2,1,0:T(2,128)(2,1)} %get-tuple-element.63) | copy-start | bytes 6291460
  420.3 3.4 copy-start.36
  431.0 285.8 %reduce-scatter.9.cloned.1.call-start = ((), (), s32[]{:S(2)}) async-start(), calls=%async_computation.13 | async-start | bytes 10485760 | tf_op jit(solution)/shard_map/reduce_scatter | solution.py:182
  491.3 16.3 %copy-start.17 = (bf16[1024,1,1024]{2,1,0:T(2,128)(2,1)S(1)}, bf16[1024,1,1024]{2,1,0:T(2,128)(2,1)}, u32[]{:S(2)}) copy-start(bf16[1024,1,1024]{2,1,0:T(2,128)(2,1)} %get-tuple-element.62) | copy-start | bytes 6291460
  514.6 291.0 %all-gather.11.cloned.1.call-start = ((), (), s32[]{:S(2)}) async-start(), calls=%async_computation.14 | async-start | bytes 5242880 | tf_op jit(solution)/shard_map/all_gather | solution.py:191
  716.8 5.3 copy-start.3
  716.8 5.3 copy-start.5
  716.8 5.3 copy-start.6
  723.9 223.0 %reduce-scatter.11.cloned.1.call-start = ((), (), s32[]{:S(2)}) async-start(), calls=%async_computation.15 | async-start | bytes 5242880 | tf_op jit(solution)/shard_map/reduce_scatter | solution.py:224
  818.8 6.3 copy-start.7
  818.8 6.3 copy-start.14
  818.8 11.9 %slice-start = ((s8[8388608]{0:T(1024)(128)(4,1)}), s8[4194304]{0:T(1024)(128)(4,1)S(1)}, s32[]{:S(2)}) async-start(s8[8388608]{0:T(1024)(128)(4,1)} %bitcast.177), calls=%async_computation.17 | async-start | bytes 8388608
  825.0 5.6 slice-start.1
  871.4 195.9 %all-reduce.4.cloned.1.call-start = ((), (), s32[]{:S(2)}) async-start(), calls=%async_computation.16 | async-start | bytes 12582912 | tf_op jit(solution)/shard_map/psum | solution.py:264
  871.6 8.2 copy-start.33
  888.8 4.0 copy-start.34
  900.7 46.1 %copy-start.26 = (f32[1024]{0:T(1024)S(1)}, f32[1024]{0:T(1024)}, u32[]{:S(2)}) copy-start(f32[1024]{0:T(1024)} %param.16) | copy-start | bytes 12292
  900.7 46.1 %copy-start.28 = (f32[512]{0:T(512)S(1)}, f32[512]{0:T(512)}, u32[]{:S(2)}) copy-start(f32[512]{0:T(512)} %copy-done.27) | copy-start | bytes 6148
  903.1 50.2 %all-to-all-start.1 = ((bf16[1,2,8,32,1024]{4,3,1,0,2:T(8,128)(2,1)}), bf16[1,2,8,32,1024]{4,3,1,0,2:T(8,128)(2,1)}, u32[]{:S(2)}, u32[]{:S(2)}) async-start(bf16[1,2,8,32,1024]{4,3,1,0,2:T(8,128)(2,1)} %copy.163), calls=%async_computation.3 | async-start | bytes 2097152 | tf_op jit(solution)/shard_map/all_to_all | solution.py:239
  948.9 8.6 copy-start.30
  948.9 8.7 copy-start.23
  953.3 168.7 %all-to-all-start.3 = ((bf16[1,2,8,32,1024]{4,3,1,0,2:T(8,128)(2,1)}), bf16[1,2,8,32,1024]{4,3,1,0,2:T(8,128)(2,1)}, u32[]{:S(2)}, u32[]{:S(2)}) async-start(bf16[1,2,8,32,1024]{4,3,1,0,2:T(8,128)(2,1)} %copy.182), calls=%async_computation.7 | async-start | bytes 2097152 | tf_op jit(solution)/shard_map/all_to_all | solution.py:246
  (18 other events, 35.5 us)
Sparse Core Ops, SparseCore 0:
  53.3 80.1 all-gather.4
  181.7 143.0 reduce-scatter.4
  328.5 81.4 all-gather.6
  412.0 79.2 all-gather.8
  493.5 75.3 reduce-scatter.6
  571.8 144.9 reduce-scatter.8
  724.0 81.4 all-gather.10
  871.5 75.2 reduce-scatter.10
  951.0 116.2 all-reduce.3
where the time goes:
time: 1150 us; the launch traced here: 1140 us
  waiting for transfers between devices  762 us (66%)
  local copies, waits for them, and re-layouts  124 us (11%)
  matrix products  105 us (9%)
  blocking collectives  79.3 us (7%)
  other arithmetic  49.2 us (4%)
  between operations  14.6 us (1%)
    reduce_scatter x1, waiting for transfers between devices, on_device(): lax.psum_scatter(jnp.dot(grad_upward, w_mlp[:, 0, :], preferred_element_t...  148 us
    reduce_scatter x1, waiting for transfers between devices, holder_pass(): lax.psum_scatter(jnp.dot(mixed, w_out, preferred_element_type=jnp.float32...  143 us
    psum x1, waiting for transfers between devices, on_device(): lax.psum(qkv_local.astype(jnp.bfloat16), 'seq').astype(jnp.float32)  106 us
    all_gather x1, waiting for transfers between devices, on_device(): attended_all = lax.all_gather(grad_attended, 'mp', axis=0, tiled=True)  81.6 us
    all_gather x1, waiting for transfers between devices, holder_pass(): normed_all = lax.all_gather(normed_one, 'mp', axis=0, tiled=True)  80.2 us
    all_gather x1, waiting for transfers between devices, on_device(): feed_all = lax.all_gather(grad_feed, 'mp', axis=0, tiled=True)  60.3 us
    reduce_scatter x1, waiting for transfers between devices, holder_pass(): lax.psum_scatter(jnp.dot(active, w_mlp[:, 1, :], preferred_element_type=j...  54.3 us
    all_gather x1, waiting for transfers between devices, holder_pass(): normed_mid = lax.all_gather(normed_two, 'mp', axis=0, tiled=True)  48.9 us
  transfers between devices with their start and end apart: 11, of which 9 were waited for; matrix products, arithmetic and copies ran while one was open for 9% of the time, Pallas kernels for 0%

commit v1 on v0

v1 whole, which is shorter than its diff:
```python
import functools

import jax
import jax.numpy as jnp
from jax import lax
from jax.experimental import pallas as pl
from jax.experimental.pallas import tpu as pltpu
from jax.sharding import PartitionSpec as P

HEAD = 64
LANES = 128
EPSILON = 1e-06
NEGATIVE = -1e30
ROOT = 0.7978845608028654
CUBE = 0.044715
SCALE = HEAD**-0.5
F32 = jnp.float32
BF16 = jnp.bfloat16
VMEM_BYTES = 50 * 1024 * 1024

NN = (((1,), (0,)), ((), ()))
NT = (((1,), (1,)), ((), ()))
TN = (((0,), (0,)), ((), ()))

ANY = pl.BlockSpec(memory_space=pl.ANY)
IN_VMEM = pl.BlockSpec(memory_space=pltpu.VMEM)
IN_SMEM = pl.BlockSpec(memory_space=pltpu.SMEM)


def mm(left, right, dims):
    return lax.dot_general(left, right, dims, preferred_element_type=F32)


def cost(flops, bytes_accessed, transcendentals=0):
    return pl.CostEstimate(
        flops=int(flops), bytes_accessed=int(bytes_accessed), transcendentals=int(transcendentals)
    )


def params(semantics=None):
    return pltpu.CompilerParams(dimension_semantics=semantics, vmem_limit_bytes=VMEM_BYTES)


def bit_lists(ranks):
    off = list(range(1, ranks.bit_length() - 1))
    return off, off[::-1]


def exchange(value, offset):
    ranks = lax.axis_size("seq")
    return lax.ppermute(value, "seq", [(i, i ^ offset) for i in range(ranks)])


def ring(value):
    depth = lax.axis_size("mp")
    cycle = [0] + list(range(1, depth, 2)) + list(range(2, depth, 2))[::-1]
    pairs = [(cycle[i], cycle[(i + 1) % depth]) for i in range(depth)]
    return lax.ppermute(value, "mp", pairs)


def joined(arrays):
    return arrays[0] if len(arrays) == 1 else jnp.concatenate(arrays, axis=0)


def gather_places(ranks, bits):
    held = [[0]]
    for bit in bits:
        flat = [i for part in held for i in part]
        held = [flat, [i | (1 << bit) for i in flat]]
    return held + [[i | 1 for i in part] for part in held]


def gather(piece, bits):
    held = [piece[None]]
    for bit in bits:
        whole = joined(held)
        held = [whole, exchange(whole, 1 << bit)]
    return held + [exchange(part, 1) for part in held]


def scatter_order(ranks, bits):
    order = []
    for j in range(ranks // 2):
        index = 0
        for place, bit in enumerate(bits):
            if (j >> (len(bits) - 1 - place)) & 1:
                index |= 1 << bit
        order.append(index)
    return order


def added(left, right):
    return (left.astype(F32) + right.astype(F32)).astype(BF16)


def scatter(keep, send, bits):
    total = added(keep, exchange(send, 1))
    for bit in bits:
        half = total.shape[0] // 2
        total = added(total[:half], exchange(total[half:], 1 << bit))
    return total[0]


def sum_everywhere(value):
    for axis in ("seq", "mp"):
        size = lax.axis_size(axis)
        step = 1
        while step < size:
            value = value + lax.ppermute(value, axis, [(i, i ^ step) for i in range(size)])
            step *= 2
    return value


def select_kernel(place_ref, tokens_ref, grads_ref, out_tokens, out_grads):
    span = tokens_ref.shape[1]
    place = place_ref[0]
    slots = place.shape[0]
    hot = (lax.broadcasted_iota(jnp.int32, (slots, span), 1) == place).astype(BF16)
    out_tokens[0] = mm(hot, tokens_ref[0], NN).astype(BF16)
    out_grads[0] = mm(hot, grads_ref[0], NN).astype(BF16)


def select_rows(place, tokens, cotangent):
    group, span, width = tokens.shape
    slots = place.shape[1]
    shape = jax.ShapeDtypeStruct((group, slots, width), BF16)
    rows = pl.BlockSpec((1, slots, width), lambda g: (g, 0, 0))
    block = pl.BlockSpec((1, span, width), lambda g: (g, 0, 0))
    return pl.pallas_call(
        select_kernel,
        grid=(group,),
        in_specs=[pl.BlockSpec((1, slots, 1), lambda g: (g, 0, 0)), block, block],
        out_specs=[rows, rows],
        out_shape=[shape, shape],
        compiler_params=params(("arbitrary",)),
        cost_estimate=cost(4 * group * slots * span * width, 4 * group * (span + slots) * width),
    )(place[:, :, None], tokens, cotangent)


def add_kernel(place_ref, base_ref, rows_ref, out_ref):
    span = base_ref.shape[1]
    place = place_ref[0]
    slots = place.shape[1]
    hot = (lax.broadcasted_iota(jnp.int32, (span, slots), 0) == place).astype(BF16)
    moved = mm(hot, rows_ref[0], NN)
    out_ref[0] = (base_ref[0].astype(F32) + moved).astype(BF16)


def add_rows(place, base, rows):
    group, span, width = base.shape
    slots = place.shape[1]
    block = pl.BlockSpec((1, span, width), lambda g: (g, 0, 0))
    return pl.pallas_call(
        add_kernel,
        grid=(group,),
        in_specs=[
            pl.BlockSpec((1, 1, slots), lambda g: (g, 0, 0)),
            block,
            pl.BlockSpec((1, slots, width), lambda g: (g, 0, 0)),
        ],
        out_specs=block,
        out_shape=jax.ShapeDtypeStruct(base.shape, BF16),
        compiler_params=params(("arbitrary",)),
        cost_estimate=cost(2 * group * slots * span * width, 4 * group * span * width),
    )(place[:, None, :], base, rows)


def start_all(copies, sems):
    started = []
    for at, (source, target) in enumerate(copies):
        copy = pltpu.make_async_copy(source, target, sems.at[at])
        copy.start()
        started.append(copy)
    return started


def attention_copies(me, sources, places, target):
    if len(sources) == 1:
        return [(sources[0], target)]
    half = len(sources) // 2
    depth = sources[0].shape[2]
    copies = []
    for side in range(2):
        for source, ids in zip(sources[side * half : (side + 1) * half], places[side]):
            for at, index in enumerate(ids):
                start = pl.multiple_of((me ^ index) * depth, depth)
                copies.append(
                    (
                        source.at[at],
                        target.at[pl.ds(2 * side, 2), pl.ds(start, depth), :],
                    )
                )
    return copies


def mlp_copies(me, sources, places, order, targets):
    half = len(sources) // 2
    copies = []
    for place, index in enumerate(order):
        for side in range(2):
            target = targets[side]
            if half == 1:
                depth = target.shape[0] // len(order)
                start = pl.multiple_of((me ^ index) * depth, depth)
                source = sources[side].at[pl.ds(start, depth), :]
            else:
                for array, ids in zip(sources[side * half : (side + 1) * half], places[side]):
                    if index in ids:
                        source = array.at[ids.index(index)]
                        depth = array.shape[1]
            copies.append((source, target.at[pl.ds(place * depth, depth), :]))
    return copies


def row_blocks(rows):
    half = rows // 3
    return (
        (0, half, 0, half),
        (half, 2 * half, 0, 2 * half),
        (2 * half, rows, 2 * half, rows),
    )


def causal(first, last, low, high):
    shape = (last - first, high - low)
    row = lax.broadcasted_iota(jnp.int32, shape, 0) + (first - low)
    return row >= lax.broadcasted_iota(jnp.int32, shape, 1)


def attention_forward_kernel(places, n_sources, has_acc, me_ref, normed_ref, *refs):
    sources, refs = refs[:n_sources], refs[n_sources:]
    if has_acc:
        acc_ref, refs = refs[0], refs[1:]
    attended_ref, heads_ref, mixed_ref, log_ref, held, sems = refs
    copies = start_all(attention_copies(me_ref[0], sources, places, held), sems)
    for copy in copies:
        copy.wait()
    rows = normed_ref.shape[0]
    width = held.shape[2]
    for c in range(3):
        heads_ref[c] = mm(normed_ref[...], held[c], NN).astype(BF16)
    lane = lax.broadcasted_iota(jnp.int32, (1, LANES), 1)
    logs = [jnp.zeros((last - first, LANES), F32) for first, last, low, high in row_blocks(rows)]
    for pair in range(width // LANES):
        lanes = slice(pair * LANES, (pair + 1) * LANES)
        for at, (first, last, low, high) in enumerate(row_blocks(rows)):
            query = heads_ref[0, first:last, lanes]
            keys = heads_ref[1, low:high, lanes]
            values = heads_ref[2, low:high, lanes]
            seen = causal(first, last, low, high)
            out = None
            for side in range(2):
                mine = (lane >= HEAD) if side else (lane < HEAD)
                scores = mm(jnp.where(mine, query, jnp.zeros_like(query)), keys, NT) * SCALE
                scores = jnp.where(seen, scores, NEGATIVE)
                peak = jnp.max(scores, axis=-1, keepdims=True)
                raised = jnp.exp(scores - peak)
                total = jnp.sum(raised, axis=-1, keepdims=True)
                weights = (raised * (1.0 / total)).astype(BF16)
                part = mm(weights, values, NN)
                out = part if out is None else jnp.where(mine, part, out)
                logs[at] = jnp.where(lane == 2 * pair + side, peak + jnp.log(total), logs[at])
            mixed_ref[first:last, lanes] = out.astype(BF16)
    for at, (first, last, low, high) in enumerate(row_blocks(rows)):
        log_ref[first:last, :] = logs[at]
    attended = mm(mixed_ref[...], held[3], NT)
    if has_acc:
        attended = attended + acc_ref[...]
    attended_ref[...] = attended


def attention_forward(me, normed, sources, places, acc):
    rows, width = normed.shape
    columns = sources[0].shape[-1]
    has_acc = acc is not None
    n_sources = len(sources)
    n_copies = 1 if n_sources == 1 else 2 * lax.axis_size("seq")
    flops = 2 * rows * width * columns * 4 + 4 * rows * rows * columns
    return pl.pallas_call(
        functools.partial(attention_forward_kernel, places, n_sources, has_acc),
        in_specs=[IN_SMEM, IN_VMEM] + [ANY] * n_sources + [IN_VMEM] * has_acc,
        out_specs=[IN_VMEM] * 4,
        out_shape=[
            jax.ShapeDtypeStruct((rows, width), F32),
            jax.ShapeDtypeStruct((3, rows, columns), BF16),
            jax.ShapeDtypeStruct((rows, columns), BF16),
            jax.ShapeDtypeStruct((rows, LANES), F32),
        ],
        scratch_shapes=[
            pltpu.VMEM((4, width, columns), BF16),
            pltpu.SemaphoreType.DMA((n_copies,)),
        ],
        input_output_aliases={2 + n_sources: 0} if has_acc else {},
        compiler_params=params(),
        cost_estimate=cost(flops, 8 * rows * width + 8 * width * columns, rows * rows * 4),
    )(me, normed, *sources, *([acc] if has_acc else []))


def attention_backward_kernel(
    places, orders, n_sources, has_acc, me_ref, grad_ref, normed_ref, heads_ref, mixed_ref, log_ref, *refs
):
    sources, refs = refs[:n_sources], refs[n_sources:]
    if has_acc:
        acc_ref, refs = refs[0], refs[1:]
    grad_normed_ref, refs = refs[0], refs[1:]
    outs, refs = refs[:4], refs[4:]
    held, grad_held, grad_heads, sems, out_sems = refs
    me = me_ref[0]
    copies = start_all(attention_copies(me, sources, places, held), sems)
    rows = normed_ref.shape[0]
    width = held.shape[2]
    depth = outs[0].shape[2]
    grad_held[3] = mm(grad_ref[...], mixed_ref[...], TN).astype(BF16)
    for copy in copies:
        copy.wait()
    grad_mixed = mm(grad_ref[...], held[3], NN).astype(BF16)
    lane = lax.broadcasted_iota(jnp.int32, (1, LANES), 1)
    for pair in range(width // LANES):
        lanes = slice(pair * LANES, (pair + 1) * LANES)
        key_parts, value_parts = [], []
        for first, last, low, high in row_blocks(rows):
            query = heads_ref[0, first:last, lanes]
            keys = heads_ref[1, low:high, lanes]
            values = heads_ref[2, low:high, lanes]
            grad_out = grad_mixed[first:last, lanes]
            logs = log_ref[first:last, :]
            seen = causal(first, last, low, high)
            grad_query = grad_keys = grad_values = None
            for side in range(2):
                mine = (lane >= HEAD) if side else (lane < HEAD)
                own_query = jnp.where(mine, query, jnp.zeros_like(query))
                own_grad = jnp.where(mine, grad_out, jnp.zeros_like(grad_out))
                log_total = jnp.sum(
                    jnp.where(lane == 2 * pair + side, logs, 0.0), axis=-1, keepdims=True
                )
                scores = jnp.where(seen, mm(own_query, keys, NT) * SCALE, NEGATIVE)
                shares = jnp.exp(scores - log_total)
                grad_weights = mm(own_grad, values, NT)
                inner = jnp.sum(shares * grad_weights, axis=-1, keepdims=True)
                grad_scores = (shares * (grad_weights - inner)).astype(BF16)
                weights = shares.astype(BF16)
                part_query = mm(grad_scores, keys, NN)
                part_keys = mm(grad_scores, own_query, TN)
                part_values = mm(weights, own_grad, TN)
                if side == 0:
                    grad_query, grad_keys, grad_values = part_query, part_keys, part_values
                else:
                    grad_query = jnp.where(mine, part_query, grad_query)
                    grad_keys = grad_keys + part_keys
                    grad_values = grad_values + part_values
            grad_heads[0, first:last, lanes] = (grad_query * SCALE).astype(BF16)
            key_parts.append(grad_keys)
            value_parts.append(grad_values)
        half = rows // 3
        for c, parts, scale in ((1, key_parts, SCALE), (2, value_parts, 1.0)):
            early = parts[0] + parts[1][:half]
            for at, value in enumerate((early, parts[1][half:], parts[2])):
                grad_heads[c, at * half : (at + 1) * half, lanes] = (value * scale).astype(BF16)
    grad_normed = mm(grad_heads[0], held[0], NT)
    for c in range(1, 3):
        grad_normed = grad_normed + mm(grad_heads[c], held[c], NT)
    if has_acc:
        grad_normed = grad_normed + acc_ref[...]
    grad_normed_ref[...] = grad_normed
    for c in range(3):
        grad_held[c] = mm(normed_ref[...], grad_heads[c], TN).astype(BF16)
    copies = []
    for side in range(2):
        for core in range(2):
            for at, index in enumerate(orders[side]):
                start = pl.multiple_of((me ^ (index | core)) * depth, depth)
                copies.append(
                    (
                        grad_held.at[pl.ds(2 * side, 2), pl.ds(start, depth), :],
                        outs[2 * side + core].at[at],
                    )
                )
    for copy in start_all(copies, out_sems):
        copy.wait()


def attention_backward(me, grad, normed, heads, mixed, logs, sources, places, orders, acc):
    rows, width = normed.shape
    columns = mixed.shape[-1]
    ranks = lax.axis_size("seq")
    has_acc = acc is not None
    n_sources = len(sources)
    n_copies = 1 if n_sources == 1 else 2 * ranks
    piece = jax.ShapeDtypeStruct((ranks // 2, 2, width // ranks, columns), BF16)
    flops = 2 * rows * width * columns * 8 + 10 * rows * rows * columns
    return pl.pallas_call(
        functools.partial(attention_backward_kernel, places, orders, n_sources, has_acc),
        in_specs=[IN_SMEM] + [IN_VMEM] * 5 + [ANY] * n_sources + [IN_VMEM] * has_acc,
        out_specs=[IN_VMEM] + [ANY] * 4,
        out_shape=[jax.ShapeDtypeStruct((rows, width), F32)] + [piece] * 4,
        scratch_shapes=[
            pltpu.VMEM((4, width, columns), BF16),
            pltpu.VMEM((4, width, columns), BF16),
            pltpu.VMEM((3, rows, columns), BF16),
            pltpu.SemaphoreType.DMA((n_copies,)),
            pltpu.SemaphoreType.DMA((2 * ranks,)),
        ],
        input_output_aliases={6 + n_sources: 0} if has_acc else {},
        compiler_params=params(),
        cost_estimate=cost(flops, 12 * rows * width + 16 * width * columns, rows * rows * 4),
    )(me, grad, normed, heads, mixed, logs, *sources, *([acc] if has_acc else []))


def mlp_kernel(places, order, orders, n_sources, has_acc, me_ref, normed_ref, grad_ref, *refs):
    sources, refs = refs[:n_sources], refs[n_sources:]
    if has_acc:
        feed_in, grad_in, refs = refs[0], refs[1], refs[2:]
    feed_ref, grad_normed_ref, refs = refs[0], refs[1], refs[2:]
    outs, refs = refs[:4], refs[4:]
    up_held, down_held, active_held, upward_held, sems = refs
    copies = start_all(
        mlp_copies(me_ref[0], sources, places, order, (up_held, down_held)), sems
    )
    hidden = up_held.shape[0]
    depth = hidden // len(order)
    step = max(depth, min(256, hidden))
    waited = 0
    for start in range(0, hidden, step):
        ready = 2 * ((start + step) // depth)
        for copy in copies[waited:ready]:
            copy.wait()
        waited = ready
        chunk = slice(start, start + step)
        upward = mm(normed_ref[...], up_held[chunk], NT)
        square = upward * upward
        bent = jnp.tanh(ROOT * upward * (1.0 + CUBE * square))
        active = (0.5 * upward * (1.0 + bent)).astype(BF16)
        slope = 0.5 * (1.0 + bent) + 0.5 * ROOT * upward * (1.0 - bent * bent) * (
            1.0 + 3.0 * CUBE * square
        )
        grad_active = mm(grad_ref[...], down_held[chunk], NT)
        grad_upward = (grad_active * slope).astype(BF16)
        active_held[:, chunk] = active
        upward_held[:, chunk] = grad_upward
        up_rows = mm(grad_upward, normed_ref[...], TN).astype(BF16)
        down_rows = mm(active, grad_ref[...], TN).astype(BF16)
        for at in range(step // depth):
            index = order[start // depth + at]
            rows = slice(at * depth, (at + 1) * depth)
            core = index & 1
            outs[core][orders[0].index(index & ~1)] = up_rows[rows]
            outs[2 + core][orders[1].index(index & ~1)] = down_rows[rows]
    feed = mm(active_held[...], down_held[...], NN)
    grad_normed = mm(upward_held[...], up_held[...], NN)
    if has_acc:
        feed = feed + feed_in[...]
        grad_normed = grad_normed + grad_in[...]
    feed_ref[...] = feed
    grad_normed_ref[...] = grad_normed


def mlp(me, normed, grad, sources, hidden, places, order, orders, acc):
    rows, width = normed.shape
    ranks = lax.axis_size("seq")
    depth = hidden // ranks
    has_acc = acc is not None
    n_sources = len(sources)
    piece = jax.ShapeDtypeStruct((ranks // 2, depth, width), BF16)
    total = jax.ShapeDtypeStruct((rows, width), F32)
    return pl.pallas_call(
        functools.partial(mlp_kernel, places, order, orders, n_sources, has_acc),
        in_specs=[IN_SMEM] + [IN_VMEM] * 2 + [ANY] * n_sources + [IN_VMEM] * (2 * has_acc),
        out_specs=[IN_VMEM] * 6,
        out_shape=[total, total] + [piece] * 4,
        scratch_shapes=[
            pltpu.VMEM((hidden, width), BF16),
            pltpu.VMEM((hidden, width), BF16),
            pltpu.VMEM((rows, hidden), BF16),
            pltpu.VMEM((rows, hidden), BF16),
            pltpu.SemaphoreType.DMA((2 * ranks,)),
        ],
        input_output_aliases={3 + n_sources: 0, 4 + n_sources: 1} if has_acc else {},
        compiler_params=params(),
        cost_estimate=cost(
            12 * rows * width * hidden, 20 * rows * width + 8 * width * hidden, rows * hidden
        ),
    )(me, normed, grad, *sources, *(acc if has_acc else []))


def place_attention_kernel(places, n_sources, me_ref, *refs):
    sources, refs = refs[:n_sources], refs[n_sources:]
    qkv_ref, out_ref, held, sems = refs
    for copy in start_all(attention_copies(me_ref[0], sources, places, held), sems):
        copy.wait()
    for c in range(3):
        qkv_ref[c] = held[c].astype(F32)
    out_ref[...] = held[3].astype(F32).T


def place_attention(me, sources, places, width):
    columns = sources[0].shape[-1]
    n_sources = len(sources)
    return pl.pallas_call(
        functools.partial(place_attention_kernel, places, n_sources),
        in_specs=[IN_SMEM] + [ANY] * n_sources,
        out_specs=[IN_VMEM] * 2,
        out_shape=[
            jax.ShapeDtypeStruct((3, width, columns), F32),
            jax.ShapeDtypeStruct((columns, width), F32),
        ],
        scratch_shapes=[
            pltpu.VMEM((4, width, columns), BF16),
            pltpu.SemaphoreType.DMA((2 * lax.axis_size("seq"),)),
        ],
        compiler_params=params(),
        cost_estimate=cost(0, 24 * width * columns),
    )(me, *sources)


def place_mlp_kernel(places, order, n_sources, me_ref, *refs):
    sources, refs = refs[:n_sources], refs[n_sources:]
    up_ref, down_ref, up_held, down_held, sems = refs
    me = me_ref[0]
    copies = mlp_copies(me, sources, places, order, (up_held, down_held))
    depth = sources[0].shape[1]
    moved = []
    for at, (source, unused) in enumerate(copies):
        start = pl.multiple_of((me ^ order[at // 2]) * depth, depth)
        moved.append((source, (up_held, down_held)[at % 2].at[pl.ds(start, depth), :]))
    for copy in start_all(moved, sems):
        copy.wait()
    up_ref[...] = up_held[...].astype(F32)
    down_ref[...] = down_held[...].astype(F32)


def place_mlp(me, sources, places, order, hidden):
    width = sources[0].shape[-1]
    n_sources = len(sources)
    whole = jax.ShapeDtypeStruct((hidden, width), F32)
    return pl.pallas_call(
        functools.partial(place_mlp_kernel, places, order, n_sources),
        in_specs=[IN_SMEM] + [ANY] * n_sources,
        out_specs=[IN_VMEM] * 2,
        out_shape=[whole, whole],
        scratch_shapes=[
            pltpu.VMEM((hidden, width), BF16),
            pltpu.VMEM((hidden, width), BF16),
            pltpu.SemaphoreType.DMA((2 * lax.axis_size("seq"),)),
        ],
        compiler_params=params(),
        cost_estimate=cost(0, 12 * hidden * width),
    )(me, *sources)


def rms_scale(values):
    return lax.rsqrt(jnp.mean(values * values, axis=-1, keepdims=True) + EPSILON)


def norm_back(grad_normed, unit_rows, scale, gain):
    scaled = gain * grad_normed
    return scale * (scaled - unit_rows * jnp.mean(unit_rows * scaled, axis=-1, keepdims=True))


def pack(first_longer, got):
    ranks, held, slots, width = got.shape
    longer = jnp.where(first_longer, got[:, 0], got[:, 1])
    shorter = jnp.where(first_longer, got[: ranks // 2, 1], got[: ranks // 2, 0])
    return jnp.concatenate(
        [longer.reshape(ranks * slots, width), shorter.reshape(ranks * slots // 2, width)]
    )


def unpack(first_longer, packed, ranks):
    rows, width = packed.shape
    half = rows // 3
    longer = packed[: 2 * half]
    shorter = jnp.concatenate([packed[2 * half :], jnp.zeros((half, width), packed.dtype)])
    both = jnp.stack(
        [
            jnp.where(first_longer, longer, shorter),
            jnp.where(first_longer, shorter, longer),
        ]
    )
    return both.reshape(1, 2, ranks, 2 * half // ranks, width)


def on_device(tokens, cotangent, lengths, routed, gain_attn, gain_mlp, router, w_qkv, w_out, w_mlp):
    group, span, width = tokens.shape
    slots = routed.shape[1]
    ranks = lax.axis_size("seq")
    depth = lax.axis_size("mp")
    held = group // ranks
    columns = w_qkv.shape[2]
    hidden = w_mlp.shape[0]
    me = lax.axis_index("seq")
    me_array = me.astype(jnp.int32)[None]
    up_bits, down_bits = bit_lists(ranks)
    places = (gather_places(ranks, up_bits), gather_places(ranks, down_bits))
    orders = (scatter_order(ranks, up_bits), scatter_order(ranks, down_bits))
    order = orders[0] + [i | 1 for i in orders[0]]

    own_attn = jnp.concatenate([w_qkv, w_out.T[None]])
    own_up, own_down = w_mlp[:, 0, :], w_mlp[:, 1, :]
    piece_attn = lax.dynamic_slice_in_dim(own_attn, me * (width // ranks), width // ranks, 1)
    piece_up = lax.dynamic_slice_in_dim(own_up, me * (hidden // ranks), hidden // ranks, 0)
    piece_down = lax.dynamic_slice_in_dim(own_down, me * (hidden // ranks), hidden // ranks, 0)
    moving = (piece_attn[:2], piece_attn[2:], piece_up, piece_down)
    attn_shards, mlp_shards = [[own_attn]], [[own_up, own_down]]
    for unused in range(1, depth):
        moving = tuple(ring(part) for part in moving)
        attn_shards.append(gather(moving[0], up_bits) + gather(moving[1], down_bits))
        mlp_shards.append(gather(moving[2], up_bits) + gather(moving[3], down_bits))

    slot = lax.broadcasted_iota(jnp.int32, routed.shape, 1)
    live = me * slots + slot < (lengths // 8)[:, None]
    place = jnp.where(live, slot * 8 + routed % 8, -1)
    chosen, chosen_grad = select_rows(place, tokens, cotangent)
    pair = lax.dynamic_slice_in_dim(lengths, me * held, held, 0)
    first_longer = pair[0] >= pair[1]

    def to_holder(value):
        return lax.all_to_all(
            value.reshape(ranks, held, slots, width), "seq", split_axis=0, concat_axis=0, tiled=True
        )

    def to_position(value):
        back = lax.all_to_all(
            unpack(first_longer, value, ranks), "seq", split_axis=2, concat_axis=0, tiled=True
        )
        return back.reshape(group, slots, width)

    picked = pack(first_longer, to_holder(chosen)).astype(F32)
    grad_rows = pack(first_longer, to_holder(chosen_grad)).astype(F32)

    scale_one = rms_scale(picked)
    unit_one = picked * scale_one
    normed_one = (unit_one * gain_attn).astype(BF16)
    gate = jax.nn.sigmoid(jnp.sum(picked * router, axis=-1, keepdims=True))
    grad_feed = (gate * grad_rows).astype(BF16)
    attended, saved = None, []
    for shard in attn_shards:
        attended, *rest = attention_forward(me_array, normed_one, shard, places, attended)
        saved.append(rest)
    middle = picked + attended
    scale_two = rms_scale(middle)
    unit_two = middle * scale_two
    normed_two = (unit_two * gain_mlp).astype(BF16)

    feed_sums, mlp_grads = None, []
    for shard in mlp_shards:
        feed, grad_normed_two, *rest = mlp(
            me_array, normed_two, grad_feed, shard, hidden, places, order, orders, feed_sums
        )
        feed_sums = (feed, grad_normed_two)
        mlp_grads.append(
            (scatter(rest[0], rest[1], up_bits), scatter(rest[2], rest[3], down_bits))
        )
    feed, grad_normed_two = feed_sums
    delta = attended + feed
    layer_out = add_rows(place, tokens, to_position((gate * delta).astype(BF16)))

    grad_logit = jnp.sum(grad_rows * delta, axis=-1, keepdims=True) * gate * (1.0 - gate)
    router_part = jnp.sum(grad_logit * picked, axis=0)
    grad_middle = norm_back(grad_normed_two, unit_two, scale_two, gain_mlp)
    mlp_gain_part = jnp.sum(grad_normed_two * unit_two, axis=0)
    grad_attended = (gate * grad_rows + grad_middle).astype(BF16)

    grad_normed_one, attn_grads = None, [None] * depth
    for k in list(range(1, depth)) + [0]:
        grad_normed_one, *rest = attention_backward(
            me_array,
            grad_attended,
            normed_one,
            *saved[k],
            attn_shards[k],
            places,
            orders,
            grad_normed_one,
        )
        attn_grads[k] = (
            scatter(rest[0], rest[1], up_bits),
            scatter(rest[2], rest[3], down_bits),
        )
    attn_gain_part = jnp.sum(grad_normed_one * unit_one, axis=0)
    grad_picked = (
        grad_middle
        + norm_back(grad_normed_one, unit_one, scale_one, gain_attn)
        + grad_logit * router
    ).astype(BF16)
    grad_tokens = add_rows(place, cotangent, to_position(grad_picked))

    def collect(parts):
        totals = parts[1 % depth]
        for k in list(range(2, depth)) + [0]:
            if depth > 1:
                totals = tuple(added(ring(t), p) for t, p in zip(totals, parts[k]))
        return gather(totals[0], up_bits) + gather(totals[1], down_bits)

    grad_up, grad_down = place_mlp(me_array, collect(mlp_grads), places, order, hidden)
    grad_qkv, grad_out = place_attention(me_array, collect(attn_grads), places, width)
    grad_mlp = jnp.stack([grad_up, grad_down], axis=1)
    small = sum_everywhere(jnp.stack([attn_gain_part, mlp_gain_part, router_part]))
    return (
        layer_out,
        grad_tokens,
        small[0],
        small[1],
        small[2],
        grad_qkv,
        grad_out,
        grad_mlp,
    )


def solution(mesh):
    placed = (
        P("mp", "seq", None),
        P("mp", "seq", None),
        P("mp"),
        P("mp", "seq"),
        P(),
        P(),
        P(),
        P(None, None, "mp"),
        P("mp", None),
        P("mp", None, None),
    )
    return jax.shard_map(
        on_device,
        mesh=mesh,
        in_specs=placed,
        out_specs=(
            P("mp", "seq", None),
            P("mp", "seq", None),
            P(),
            P(),
            P(),
            P(None, None, "mp"),
            P("mp", None),
            P("mp", None, None),
        ),
        check_vma=False,
    )
```

time: 1150 us -> 611 us (0.53)
  waiting for transfers between devices: 762 us -> 174 us
  Pallas kernels: 0 us -> 179 us
  starting transfers between devices: 9.25 us -> 142 us
  matrix products: 105 us -> 0 us
  blocking collectives: 79.3 us -> 0 us
  local copies, waits for them, and re-layouts: 124 us -> 51.6 us
    reduce_scatter x4 -> x0, waiting for transfers between devices: 385 us -> none  [the longest x1 148 us: on_device(): lax.psum_scatter(jnp.dot(grad_upward, w_mlp[:, 0, :], preferred_element_t...]
    all_gather x4 -> x0, waiting for transfers between devices: 271 us -> none  [the longest x1 81.6 us: on_device(): attended_all = lax.all_gather(grad_attended, 'mp', axis=0, tiled=True)]
    pallas_call x0 -> x17, Pallas kernels: none -> 179 us  [the longest x4 50.1 us: attention_backward(): pl.pallas_call(functools.partial(attention_backward_kernel, places, order...]
    ppermute x0 -> x141, waiting for transfers between devices: none -> 174 us  [the longest x112 132 us: exchange(): return lax.ppermute(value, 'seq', [(i, i ^ offset) for i in range(ranks)])]
    ppermute x0 -> x141, starting transfers between devices: none -> 125 us  [the longest x112 86.8 us: exchange(): return lax.ppermute(value, 'seq', [(i, i ^ offset) for i in range(ranks)])]
    psum x1 -> x0, waiting for transfers between devices: 106 us -> none  [on_device(): lax.psum(qkv_local.astype(jnp.bfloat16), 'seq').astype(jnp.float32)]
    dot_general x20 -> x0, matrix products: 105 us -> none  [the longest x1 14.3 us: on_device(): lax.dot_general(feed_all, w_mlp[:, 1, :], CONTRACT_COLS, preferred_elemen...]
    all_to_all x2 -> x0, blocking collectives: 39.7 us -> none  [the longest x1 20.3 us: on_device(): lax.all_to_all(chosen.reshape(ranks, held, 1, slots, width), 'seq', split...]
  transfers between devices with their start and end apart: 11 -> 145, of which waited for: 9 -> 47; matrix products, arithmetic and copies ran while one was open for 9% -> 11% of each run, Pallas kernels for 0% -> 26%
where the time goes in v1:
time: 611 us; the launch traced here: 601 us
  Pallas kernels  179 us (29%)
  waiting for transfers between devices  174 us (28%)
  starting transfers between devices  142 us (23%)
  local copies, waits for them, and re-layouts  51.6 us (8%)
  other arithmetic  49.9 us (8%)
    ppermute x112, waiting for transfers between devices, exchange(): return lax.ppermute(value, 'seq', [(i, i ^ offset) for i in range(ranks)])  132 us
    ppermute x112, starting transfers between devices, exchange(): return lax.ppermute(value, 'seq', [(i, i ^ offset) for i in range(ranks)])  86.8 us
    pallas_call x4, Pallas kernels, attention_backward(): pl.pallas_call(functools.partial(attention_backward_kernel, places, order...  50.1 us
    pallas_call x4, Pallas kernels, mlp(): pl.pallas_call(functools.partial(mlp_kernel, places, order, orders, n_sou...  46.3 us
    unnamed x256, local copies, waits for them, and re-layouts  39.4 us
    ppermute x24, starting transfers between devices, ring(): return lax.ppermute(value, 'mp', pairs)  32.4 us
    pallas_call x4, Pallas kernels, attention_forward(): pl.pallas_call(functools.partial(attention_forward_kernel, places, n_sour...  31.2 us
    pallas_call x2, Pallas kernels, add_rows(): pl.pallas_call(add_kernel, grid=(group,), in_specs=[pl.BlockSpec((1, 1, s...  27.3 us
  transfers between devices with their start and end apart: 145, of which 47 were waited for; matrix products, arithmetic and copies ran while one was open for 11% of the time, Pallas kernels for 26%

profile of v1, /device:TPU:0, one launch (start us, length us, event | category | flops | bytes accessed | tf_op | source)
XLA Modules:
  0.0 601.5 jit_solution(3442482819303310943)
XLA Ops:
  2.3 14.2 %shard_map.161 = (bf16[16,32,1024]{2,1,0:T(8,128)(2,1)}, bf16[16,32,1024]{2,1,0:T(8,128)(2,1)}) custom-call(s32[16,32,1]{2,1,0:T(8,128)S(1)} %copy.40.place_ref, bf16[16,256,1024]{2,1,0:T(8,128)(2,1)} %base_ref.2, bf16[16,256,1024]{2,1,0:T(8,128)(2,1)} %base_ref.3), custom_call_target="tpu_custom_call" | custom-call | flops 536870912 | bytes 18874368 | tf_op jit(solution)/shard_map/pallas_call | solution.py:129
  16.5 5.3 all-to-all-start
  27.2 9.0 %fusion.56 = (bf16[1024,1,1024]{2,1,0:T(2,128)(2,1)S(1)}, bf16[1024,1,1024]{2,1,0:T(2,128)(2,1)S(1)}) fusion(bf16[1024,2,1024]{2,1,0:T(2,128)(2,1)} %param.19), kind=kLoop, calls=%fused_computation.179 | loop fusion | bytes 8388608 | tf_op jit(solution)/shard_map/slice | solution.py:598
  49.9 4.5 copy.53
  82.4 10.8 %collective-permute-done.3 = bf16[1,2,128,256]{3,2,1,0:T(8,128)(2,1)S(1)} collective-permute-done((bf16[1,2,128,256]{3,2,1,0:T(8,128)(2,1)}, bf16[1,2,128,256]{3,2,1,0:T(8,128)(2,1)S(1)}, u32[]{:S(2)}, u32[]{:S(2)}) %collective-permute-start.3) | collective-permute-done | bytes 131104 | tf_op jit(solution)/shard_map/ppermute | solution.py:51
  98.4 8.3 %collective-permute-done.48 = bf16[1,128,1024]{2,1,0:T(8,128)(2,1)S(1)} collective-permute-done((bf16[1,128,1024]{2,1,0:T(8,128)(2,1)S(1)}, bf16[1,128,1024]{2,1,0:T(8,128)(2,1)S(1)}, u32[]{:S(2)}, u32[]{:S(2)}) %collective-permute-start.48) | collective-permute-done | bytes 262176 | tf_op jit(solution)/shard_map/ppermute | solution.py:51
  124.6 5.8 shard_map.162
  136.2 8.6 %shard_map.163 = (f32[384,1024]{1,0:T(8,128)}, bf16[3,384,256]{2,1,0:T(8,128)(2,1)S(1)}, bf16[384,256]{1,0:T(8,128)(2,1)S(1)}, f32[384,128]{1,0:T(8,128)S(1)}) custom-call(s32[1]{0:T(128)} %bitcast.6.me_ref, bf16[384,1024]{1,0:T(8,128)(2,1)S(1)} %fusion.8.normed_ref, ...), custom_call_target="tpu_custom_call", output_to_operand_aliasing={{0}: (10, {})} | custom-call | flops 956301312 | bytes 5242880 | tf_op jit(solution)/shard_map/pallas_call | solution.py:279
  147.0 8.0 %shard_map.164 = (f32[384,1024]{1,0:T(8,128)}, bf16[3,384,256]{2,1,0:T(8,128)(2,1)S(1)}, bf16[384,256]{1,0:T(8,128)(2,1)S(1)}, f32[384,128]{1,0:T(8,128)S(1)}) custom-call(s32[1]{0:T(128)} %bitcast.6.me_ref, bf16[384,1024]{1,0:T(8,128)(2,1)S(1)} %fusion.8.normed_ref, ...), custom_call_target="tpu_custom_call", output_to_operand_aliasing={{0}: (10, {})} | custom-call | flops 956301312 | bytes 5242880 | tf_op jit(solution)/shard_map/pallas_call | solution.py:279
  155.7 8.8 %shard_map.165 = (f32[384,1024]{1,0:T(8,128)}, bf16[3,384,256]{2,1,0:T(8,128)(2,1)S(1)}, bf16[384,256]{1,0:T(8,128)(2,1)S(1)}, f32[384,128]{1,0:T(8,128)S(1)}) custom-call(s32[1]{0:T(128)} %bitcast.6.me_ref, bf16[384,1024]{1,0:T(8,128)(2,1)S(1)} %fusion.8.normed_ref, ...), custom_call_target="tpu_custom_call", output_to_operand_aliasing={{0}: (10, {})} | custom-call | flops 956301312 | bytes 5242880 | tf_op jit(solution)/shard_map/pallas_call | solution.py:279
  175.0 9.6 %collective-permute-done.45.refs_1_ = bf16[2,128,1024]{2,1,0:T(8,128)(2,1)S(1)} collective-permute-done((bf16[2,128,1024]{2,1,0:T(8,128)(2,1)S(1)}, bf16[2,128,1024]{2,1,0:T(8,128)(2,1)S(1)}, u32[]{:S(2)}, u32[]{:S(2)}) %collective-permute-start.45) | collective-permute-done | bytes 524320 | tf_op jit(solution)/shard_map/ppermute | solution.py:51
  189.9 10.4 %shard_map.166 = (f32[384,1024]{1,0:T(8,128)}, f32[384,1024]{1,0:T(8,128)}, bf16[4,128,1024]{2,1,0:T(8,128)(2,1)S(1)}, bf16[4,128,1024]{2,1,0:T(8,128)(2,1)}, bf...) custom-call(s32[1]{0:T(128)} %bitcast.6.me_ref, bf16[384,1024]{1,0:T(8,128)(2,1)S(1)} %multiply_convert_fusion.1.normed_ref, ...), custom_call_target="tpu_custom_call" | custom-call | flops 4831838208 | bytes 16252928 | tf_op jit(solution)/shard_map/pallas_call | solution.py:465
  201.6 11.9 %shard_map.167 = (f32[384,1024]{1,0:T(8,128)}, f32[384,1024]{1,0:T(8,128)}, bf16[4,128,1024]{2,1,0:T(8,128)(2,1)}, bf16[4,128,1024]{2,1,0:T(8,128)(2,1)}, bf16[4...) custom-call(s32[1]{0:T(128)} %bitcast.6.me_ref, ...), custom_call_target="tpu_custom_call", output_to_operand_aliasing={{0}: (11, {}), {1}: (12, {})} | custom-call | flops 4831838208 | bytes 16252928 | tf_op jit(solution)/shard_map/pallas_call | solution.py:465
  214.0 11.6 %shard_map.168 = (f32[384,1024]{1,0:T(8,128)}, f32[384,1024]{1,0:T(8,128)}, bf16[4,128,1024]{2,1,0:T(8,128)(2,1)}, bf16[4,128,1024]{2,1,0:T(8,128)(2,1)}, bf16[4...) custom-call(s32[1]{0:T(128)} %bitcast.6.me_ref, ...), custom_call_target="tpu_custom_call", output_to_operand_aliasing={{0}: (11, {}), {1}: (12, {})} | custom-call | flops 4831838208 | bytes 16252928 | tf_op jit(solution)/shard_map/pallas_call | solution.py:465
  226.3 12.5 %shard_map.169 = (f32[384,1024]{1,0:T(8,128)}, f32[384,1024]{1,0:T(8,128)}, bf16[4,128,1024]{2,1,0:T(8,128)(2,1)}, bf16[4,128,1024]{2,1,0:T(8,128)(2,1)}, bf16[4...) custom-call(s32[1]{0:T(128)} %bitcast.6.me_ref, ...), custom_call_target="tpu_custom_call", output_to_operand_aliasing={{0}: (11, {}), {1}: (12, {})} | custom-call | flops 4831838208 | bytes 16252928 | tf_op jit(solution)/shard_map/pallas_call | solution.py:465
  244.1 12.3 %shard_map.171 = (f32[384,1024]{1,0:T(8,128)}, bf16[4,2,128,256]{3,2,1,0:T(8,128)(2,1)S(1)}, bf16[4,2,128,256]{3,2,1,0:T(8,128)(2,1)S(1)}, bf16[4,2,128,256]{3,2,1,0:T(8,128)(2,1)S(1)}, bf16[4,2,128,256]{3,2,1,0:T(8,128)(2,1)}) custom-call(s32[1]{0:T(128)} %bitcast.6.me_ref, bf16[384,1024]{1,0:T(8,128)(2,1)} %fusion.6.grad_ref, bf16[384,1024]{1,0:T(8,128)(2,1)} %copy-done.2, ...), custom_call_target="tpu_custom_call" | custom-call | flops 1988100096 | bytes 8912896 | tf_op jit(solution)/shard_map/pallas_call | solution.py:391
  258.1 13.2 %shard_map.172 = (f32[384,1024]{1,0:T(8,128)}, bf16[4,2,128,256]{3,2,1,0:T(8,128)(2,1)S(1)}, bf16[4,2,128,256]{3,2,1,0:T(8,128)(2,1)S(1)}, bf16[4,2,128,256]{3,2,1,0:T(8,128)(2,1)S(1)}, bf16[4,2,128,256]{3,2,1,0:T(8,128)(2,1)}) custom-call(s32[1]{0:T(128)} %bitcast.6.me_ref, bf16[384,1024]{1,0:T(8,128)(2,1)} %fusion.6.grad_ref, ...), custom_call_target="tpu_custom_call", output_to_operand_aliasing={{0}: (14, {})} | custom-call | flops 1988100096 | bytes 8912896 | tf_op jit(solution)/shard_map/pallas_call | solution.py:391
  273.8 13.2 %shard_map.173 = (f32[384,1024]{1,0:T(8,128)}, bf16[4,2,128,256]{3,2,1,0:T(8,128)(2,1)S(1)}, bf16[4,2,128,256]{3,2,1,0:T(8,128)(2,1)S(1)}, bf16[4,2,128,256]{3,2,1,0:T(8,128)(2,1)S(1)}, bf16[4,2,128,256]{3,2,1,0:T(8,128)(2,1)}) custom-call(s32[1]{0:T(128)} %bitcast.6.me_ref, bf16[384,1024]{1,0:T(8,128)(2,1)} %fusion.6.grad_ref, ...), custom_call_target="tpu_custom_call", output_to_operand_aliasing={{0}: (14, {})} | custom-call | flops 1988100096 | bytes 8912896 | tf_op jit(solution)/shard_map/pallas_call | solution.py:391
  289.9 11.4 %shard_map.174 = (f32[384,1024]{1,0:T(8,128)}, bf16[4,2,128,256]{3,2,1,0:T(8,128)(2,1)S(1)}, bf16[4,2,128,256]{3,2,1,0:T(8,128)(2,1)S(1)}, bf16[4,2,128,256]{3,2...) custom-call(s32[1]{0:T(128)} %bitcast.6.me_ref, bf16[384,1024]{1,0:T(8,128)(2,1)S(1)} %copy-done.5, ...), custom_call_target="tpu_custom_call", output_to_operand_aliasing={{0}: (7, {})} | custom-call | flops 1988100096 | bytes 8912896 | tf_op jit(solution)/shard_map/pallas_call | solution.py:391
  323.7 12.3 %collective-permute-done.135 = bf16[2,128,1024]{2,1,0:T(8,128)(2,1)S(1)} collective-permute-done((bf16[2,128,1024]{2,1,0:T(8,128)(2,1)S(1)}, bf16[2,128,1024]{2,1,0:T(8,128)(2,1)S(1)}, u32[]{:S(2)}, u32[]{:S(2)}) %collective-permute-start.135) | collective-permute-done | bytes 524320 | tf_op jit(solution)/shard_map/ppermute | solution.py:51
  348.1 5.0 collective-permute-done.93
  360.0 4.3 collective-permute-done.85
  372.4 6.0 collective-permute-done.70
  396.9 7.3 %collective-permute-done.67 = bf16[1,2,128,256]{3,2,1,0:T(8,128)(2,1)S(1)} collective-permute-done((bf16[1,2,128,256]{3,2,1,0:T(8,128)(2,1)S(1)}, bf16[1,2,128,256]{3,2,1,0:T(8,128)(2,1)S(1)}, u32[]{:S(2)}, u32[]{:S(2)}) %collective-permute-start.67) | collective-permute-done | bytes 131104 | tf_op jit(solution)/shard_map/ppermute | solution.py:51
  409.7 8.4 %collective-permute-done.104 = bf16[2,128,1024]{2,1,0:T(8,128)(2,1)S(1)} collective-permute-done((bf16[2,128,1024]{2,1,0:T(8,128)(2,1)S(1)}, bf16[2,128,1024]{2,1,0:T(8,128)(2,1)S(1)}, u32[]{:S(2)}, u32[]{:S(2)}) %collective-permute-start.104) | collective-permute-done | bytes 524320 | tf_op jit(solution)/shard_map/ppermute | solution.py:51
  440.2 13.0 %collective-permute-done.124 = bf16[1,128,1024]{2,1,0:T(8,128)(2,1)S(1)} collective-permute-done((bf16[1,128,1024]{2,1,0:T(8,128)(2,1)S(1)}, bf16[1,128,1024]{2,1,0:T(8,128)(2,1)S(1)}, u32[]{:S(2)}, u32[]{:S(2)}) %collective-permute-start.124) | collective-permute-done | bytes 262176 | tf_op jit(solution)/shard_map/ppermute | solution.py:51
  513.5 14.2 %collective-permute-done.62 = f32[3,1024]{1,0:T(4,128)S(1)} collective-permute-done((f32[3,1024]{1,0:T(4,128)S(1)}, f32[3,1024]{1,0:T(4,128)S(1)}, u32[]{:S(2)}, u32[]{:S(2)}) %collective-permute-start.62) | collective-permute-done | bytes 12320 | tf_op jit(solution)/shard_map/ppermute | solution.py:109
  546.7 13.6 %shard_map.175 = bf16[16,256,1024]{2,1,0:T(8,128)(2,1)} custom-call(s32[16,1,32]{2,1,0:T(1,128)S(1)} %bitcast.152, bf16[16,256,1024]{2,1,0:T(8,128)(2,1)} %base_ref.3, bf16[16,32,1024]{2,1,0:T(8,128)(2,1)S(1)} %bitcast.150), custom_call_target="tpu_custom_call" | custom-call | flops 268435456 | bytes 16777216 | tf_op jit(solution)/shard_map/pallas_call | solution.py:153
  560.4 13.7 %shard_map.170 = bf16[16,256,1024]{2,1,0:T(8,128)(2,1)} custom-call(s32[16,1,32]{2,1,0:T(1,128)S(1)} %bitcast.153, bf16[16,256,1024]{2,1,0:T(8,128)(2,1)} %base_ref.2, bf16[16,32,1024]{2,1,0:T(8,128)(2,1)S(1)} %bitcast.151), custom_call_target="tpu_custom_call" | custom-call | flops 268435456 | bytes 16777216 | tf_op jit(solution)/shard_map/pallas_call | solution.py:153
  578.1 5.6 shard_map.177
  583.8 4.3 pad_maximum_fusion
  588.1 12.9 %copy.48 = f32[1024,2,1024]{2,1,0:T(2,128)} copy(f32[1024,2,1024]{2,0,1:T(8,128)S(1)} %pad_maximum_fusion) | data formatting | bytes 16777216
  (673 shorter events, 286.7 us)
Async XLA Ops:
  16.5 54.6 %all-to-all-start = ((bf16[8,2,32,1024]{3,2,1,0:T(8,128)(2,1)}), bf16[8,2,32,1024]{3,2,1,0:T(8,128)(2,1)S(1)}, u32[]{:S(2)}, u32[]{:S(2)}) async-start(bf16[8,2,32,1024]{3,2,1,0:T(8,128)(2,1)} %bitcast.3), calls=%async_computation | async-start | bytes 2097152 | tf_op jit(solution)/shard_map/all_to_all | solution.py:617
  64.7 28.5 %collective-permute-start.38 = (bf16[128,1024]{1,0:T(8,128)(2,1)S(1)}, bf16[128,1024]{1,0:T(8,128)(2,1)S(1)}, u32[]{:S(2)}, u32[]{:S(2)}) collective-permute-start(bf16[128,1024]{1,0:T(8,128)(2,1)S(1)} %collective-permute-done.37), channel_id=1, source_target_pairs={{0,1},{1,3},{3,2},{2,0},{4,5},{5,7},{7,6},{6,4},{8,9},{9,11},{11,1... | collective-permute-start | bytes 786440 | tf_op jit(solution)/shard_map/ppermute | solution.py:58
  71.1 37.9 %all-to-all-start.1 = ((bf16[8,2,32,1024]{3,2,1,0:T(8,128)(2,1)}), bf16[8,2,32,1024]{3,2,1,0:T(8,128)(2,1)}, u32[]{:S(2)}, u32[]{:S(2)}) async-start(bf16[8,2,32,1024]{3,2,1,0:T(8,128)(2,1)} %bitcast.15), calls=%async_computation.1 | async-start | bytes 2097152 | tf_op jit(solution)/shard_map/all_to_all | solution.py:617
  80.6 30.6 %collective-permute-start.23 = (bf16[2,2,128,256]{3,2,1,0:T(8,128)(2,1)S(1)}, bf16[2,2,128,256]{3,2,1,0:T(8,128)(2,1)S(1)}, u32[]{:S(2)}, u32[]{:S(2)}) collective-permute-start(bf16[2,2,128,256]{3,2,1,0:T(8,128)(2,1)S(1)} %pad_maximum_fusion.18.refs_0_), channel_id=1, source_target_pairs={{0,16},{4,20},{8,24},{12,28},{16,0},{20,4},{24,8},{28,12},{1,17},{... | collective-permute-start | bytes 786440 | tf_op jit(solution)/shard_map/ppermute | solution.py:51
  134.3 30.3 %collective-permute-start.39 = (bf16[128,1024]{1,0:T(8,128)(2,1)S(1)}, bf16[128,1024]{1,0:T(8,128)(2,1)S(1)}, u32[]{:S(2)}, u32[]{:S(2)}) collective-permute-start(bf16[128,1024]{1,0:T(8,128)(2,1)S(1)} %copy-done.109), channel_id=1, source_target_pairs={{0,1},{1,3},{3,2},{2,0},{4,5},{5,7},{7,6},{6,4},{8,9},{9,11},{11,1... | collective-permute-start | bytes 786440 | tf_op jit(solution)/shard_map/ppermute | solution.py:58
  134.4 30.5 %collective-permute-start.33 = (bf16[1,128,1024]{2,1,0:T(8,128)(2,1)S(1)}, bf16[1,128,1024]{2,1,0:T(8,128)(2,1)S(1)}, u32[]{:S(2)}, u32[]{:S(2)}) collective-permute-start(bf16[1,128,1024]{2,1,0:T(8,128)(2,1)S(1)} %bitcast.194), channel_id=1, source_target_pairs={{0,8},{4,12},{8,0},{12,4},{16,24},{20,28},{24,16},{28,20},{1,9},{5... | collective-permute-start | bytes 786440 | tf_op jit(solution)/shard_map/ppermute | solution.py:51
  200.4 25.3 %collective-permute-start.35 = (bf16[2,128,1024]{2,1,0:T(8,128)(2,1)S(1)}, bf16[2,128,1024]{2,1,0:T(8,128)(2,1)}, u32[]{:S(2)}, u32[]{:S(2)}) collective-permute-start(bf16[2,128,1024]{2,1,0:T(8,128)(2,1)S(1)} %pad_maximum_fusion.6.refs_0_), channel_id=1, source_target_pairs={{0,4},{4,0},{8,12},{12,8},{16,20},{20,16},{24,28},{28,24},{1,5},{5... | collective-permute-start | bytes 1572872 | tf_op jit(solution)/shard_map/ppermute | solution.py:51
  200.9 24.9 %collective-permute-start.42 = (bf16[2,128,1024]{2,1,0:T(8,128)(2,1)S(1)}, bf16[2,128,1024]{2,1,0:T(8,128)(2,1)}, u32[]{:S(2)}, u32[]{:S(2)}) collective-permute-start(bf16[2,128,1024]{2,1,0:T(8,128)(2,1)S(1)} %pad_maximum_fusion.7.refs_4_), channel_id=1, source_target_pairs={{0,4},{4,0},{8,12},{12,8},{16,20},{20,16},{24,28},{28,24},{1,5},{5... | collective-permute-start | bytes 1572872 | tf_op jit(solution)/shard_map/ppermute | solution.py:51
  201.0 25.2 %collective-permute-start.36 = (bf16[2,128,1024]{2,1,0:T(8,128)(2,1)}, bf16[2,128,1024]{2,1,0:T(8,128)(2,1)}, u32[]{:S(2)}, u32[]{:S(2)}) collective-permute-start(bf16[2,128,1024]{2,1,0:T(8,128)(2,1)} %collective-permute-done.34.refs_1_), channel_id=1, source_target_pairs={{0,4},{4,0},{8,12},{12,8},{16,20},{20,16},{24,28},{28,24},{1,5},{5... | collective-permute-start | bytes 1572872 | tf_op jit(solution)/shard_map/ppermute | solution.py:51
  201.4 24.9 %collective-permute-start.43 = (bf16[2,128,1024]{2,1,0:T(8,128)(2,1)}, bf16[2,128,1024]{2,1,0:T(8,128)(2,1)}, u32[]{:S(2)}, u32[]{:S(2)}) collective-permute-start(bf16[2,128,1024]{2,1,0:T(8,128)(2,1)} %collective-permute-done.41.refs_5_), channel_id=1, source_target_pairs={{0,4},{4,0},{8,12},{12,8},{16,20},{20,16},{24,28},{28,24},{1,5},{5... | collective-permute-start | bytes 1572872 | tf_op jit(solution)/shard_map/ppermute | solution.py:51
  213.5 97.6 %collective-permute-start.134 = (bf16[4,128,1024]{2,1,0:T(8,128)(2,1)}, bf16[4,128,1024]{2,1,0:T(8,128)(2,1)}, u32[]{:S(2)}, u32[]{:S(2)}) collective-permute-start(bf16[4,128,1024]{2,1,0:T(8,128)(2,1)} %get-tuple-element.137), channel_id=1, source_target_pairs={{0,4},{4,0},{8,12},{12,8},{16,20},{20,16},{24,28},{28,24},{1,5},{5... | collective-permute-start | bytes 3145736 | tf_op jit(solution)/shard_map/ppermute | solution.py:51
  225.6 88.0 %collective-permute-start.115 = (bf16[4,128,1024]{2,1,0:T(8,128)(2,1)}, bf16[4,128,1024]{2,1,0:T(8,128)(2,1)}, u32[]{:S(2)}, u32[]{:S(2)}) collective-permute-start(bf16[4,128,1024]{2,1,0:T(8,128)(2,1)} %get-tuple-element.129), channel_id=1, source_target_pairs={{0,4},{4,0},{8,12},{12,8},{16,20},{20,16},{24,28},{28,24},{1,5},{5... | collective-permute-start | bytes 3145736 | tf_op jit(solution)/shard_map/ppermute | solution.py:51
  225.8 115.1 %collective-permute-start.122 = (bf16[4,128,1024]{2,1,0:T(8,128)(2,1)}, bf16[4,128,1024]{2,1,0:T(8,128)(2,1)}, u32[]{:S(2)}, u32[]{:S(2)}) collective-permute-start(bf16[4,128,1024]{2,1,0:T(8,128)(2,1)} %get-tuple-element.131), channel_id=1, source_target_pairs={{0,4},{4,0},{8,12},{12,8},{16,20},{20,16},{24,28},{28,24},{1,5},{5... | collective-permute-start | bytes 3145736 | tf_op jit(solution)/shard_map/ppermute | solution.py:51
  226.2 117.6 %collective-permute-start.103 = (bf16[4,128,1024]{2,1,0:T(8,128)(2,1)}, bf16[4,128,1024]{2,1,0:T(8,128)(2,1)}, u32[]{:S(2)}, u32[]{:S(2)}) collective-permute-start(bf16[4,128,1024]{2,1,0:T(8,128)(2,1)} %get-tuple-element.123), channel_id=1, source_target_pairs={{0,4},{4,0},{8,12},{12,8},{16,20},{20,16},{24,28},{28,24},{1,5},{5... | collective-permute-start | bytes 3145736 | tf_op jit(solution)/shard_map/ppermute | solution.py:51
  289.5 29.6 %collective-permute-start.92 = (bf16[4,2,128,256]{3,2,1,0:T(8,128)(2,1)}, bf16[4,2,128,256]{3,2,1,0:T(8,128)(2,1)}, u32[]{:S(2)}, u32[]{:S(2)}) collective-permute-start(bf16[4,2,128,256]{3,2,1,0:T(8,128)(2,1)} %get-tuple-element.117), channel_id=1, source_target_pairs={{0,4},{4,0},{8,12},{12,8},{16,20},{20,16},{24,28},{28,24},{1,5},{5... | collective-permute-start | bytes 1572872 | tf_op jit(solution)/shard_map/ppermute | solution.py:51
  306.4 200.9 %all-to-all-start.3 = ((bf16[1,2,8,32,1024]{4,3,1,0,2:T(8,128)(2,1)}), bf16[1,2,8,32,1024]{4,3,1,0,2:T(8,128)(2,1)S(1)}, u32[]{:S(2)}, u32[]{:S(2)}) async-start(bf16[1,2,8,32,1024]{4,3,1,0,2:T(8,128)(2,1)} %pad_maximum_fusion.3), calls=%async_computation.3 | async-start | bytes 2097152 | tf_op jit(solution)/shard_map/all_to_all | solution.py:622
  318.0 71.3 %collective-permute-start.126 = (bf16[4,128,1024]{2,1,0:T(8,128)(2,1)S(1)}, bf16[4,128,1024]{2,1,0:T(8,128)(2,1)S(1)}, u32[]{:S(2)}, u32[]{:S(2)}) collective-permute-start(bf16[4,128,1024]{2,1,0:T(8,128)(2,1)S(1)} %copy-done.122), channel_id=1, source_target_pairs={{0,4},{4,0},{8,12},{12,8},{16,20},{20,16},{24,28},{28,24},{1,5},{5... | collective-permute-start | bytes 3145736 | tf_op jit(solution)/shard_map/ppermute | solution.py:51
  339.8 50.3 %collective-permute-start.107 = (bf16[4,128,1024]{2,1,0:T(8,128)(2,1)S(1)}, bf16[4,128,1024]{2,1,0:T(8,128)(2,1)S(1)}, u32[]{:S(2)}, u32[]{:S(2)}) collective-permute-start(bf16[4,128,1024]{2,1,0:T(8,128)(2,1)S(1)} %copy-done.120), channel_id=1, source_target_pairs={{0,4},{4,0},{8,12},{12,8},{16,20},{20,16},{24,28},{28,24},{1,5},{5... | collective-permute-start | bytes 3145736 | tf_op jit(solution)/shard_map/ppermute | solution.py:51
  341.2 63.8 %collective-permute-start.130 = (bf16[4,128,1024]{2,1,0:T(8,128)(2,1)S(1)}, bf16[4,128,1024]{2,1,0:T(8,128)(2,1)S(1)}, u32[]{:S(2)}, u32[]{:S(2)}) collective-permute-start(bf16[4,128,1024]{2,1,0:T(8,128)(2,1)S(1)} %copy-done.121), channel_id=1, source_target_pairs={{0,4},{4,0},{8,12},{12,8},{16,20},{20,16},{24,28},{28,24},{1,5},{5... | collective-permute-start | bytes 3145736 | tf_op jit(solution)/shard_map/ppermute | solution.py:51
  388.0 122.8 %collective-permute-start.61 = (f32[3,1024]{1,0:T(4,128)}, f32[3,1024]{1,0:T(4,128)}, u32[]{:S(2)}, u32[]{:S(2)}) collective-permute-start(f32[3,1024]{1,0:T(4,128)} %fusion.55), channel_id=1, source_target_pairs={{0,8},{4,12},{8,0},{12,4},{16,24},{20,28},{24,16},{28,20},{1,9},{5... | collective-permute-start | bytes 36872 | tf_op jit(solution)/shard_map/ppermute | solution.py:109
  405.1 24.9 %collective-permute-start.94 = (bf16[1,2,128,256]{3,2,1,0:T(8,128)(2,1)S(1)}, bf16[1,2,128,256]{3,2,1,0:T(8,128)(2,1)S(1)}, u32[]{:S(2)}, u32[]{:S(2)}) collective-permute-start(bf16[1,2,128,256]{3,2,1,0:T(8,128)(2,1)S(1)} %slice.384), channel_id=1, source_target_pairs={{0,8},{4,12},{8,0},{12,4},{16,24},{20,28},{24,16},{28,20},{1,9},{5... | collective-permute-start | bytes 393224 | tf_op jit(solution)/shard_map/ppermute | solution.py:51
  429.9 27.6 %collective-permute-start.131 = (bf16[2,128,1024]{2,1,0:T(8,128)(2,1)S(1)}, bf16[2,128,1024]{2,1,0:T(8,128)(2,1)S(1)}, u32[]{:S(2)}, u32[]{:S(2)}) collective-permute-start(bf16[2,128,1024]{2,1,0:T(8,128)(2,1)S(1)} %slice.414), channel_id=1, source_target_pairs={{0,16},{4,20},{8,24},{12,28},{16,0},{20,4},{24,8},{28,12},{1,17},{... | collective-permute-start | bytes 1572872 | tf_op jit(solution)/shard_map/ppermute | solution.py:51
  498.5 34.5 %collective-permute-start.80 = (bf16[1,2,128,256]{3,2,1,0:T(8,128)(2,1)S(1)}, bf16[1,2,128,256]{3,2,1,0:T(8,128)(2,1)}, u32[]{:S(2)}, u32[]{:S(2)}) collective-permute-start(bf16[1,2,128,256]{3,2,1,0:T(8,128)(2,1)S(1)} %fusion.50), channel_id=1, source_target_pairs={{0,8},{4,12},{8,0},{12,4},{16,24},{20,28},{24,16},{28,20},{1,9},{5... | collective-permute-start | bytes 393224 | tf_op jit(solution)/shard_map/ppermute | solution.py:51
  500.1 36.8 %collective-permute-start.100 = (bf16[2,2,128,256]{3,2,1,0:T(8,128)(2,1)S(1)}, bf16[2,2,128,256]{3,2,1,0:T(8,128)(2,1)}, u32[]{:S(2)}, u32[]{:S(2)}) collective-permute-start(bf16[2,2,128,256]{3,2,1,0:T(8,128)(2,1)S(1)} %pad_maximum_fusion.21.refs_4_), channel_id=1, source_target_pairs={{0,8},{4,12},{8,0},{12,4},{16,24},{20,28},{24,16},{28,20},{1,9},{5... | collective-permute-start | bytes 786440 | tf_op jit(solution)/shard_map/ppermute | solution.py:51
  504.9 39.1 %collective-permute-start.138 = (bf16[2,128,1024]{2,1,0:T(8,128)(2,1)S(1)}, bf16[2,128,1024]{2,1,0:T(8,128)(2,1)}, u32[]{:S(2)}, u32[]{:S(2)}) collective-permute-start(bf16[2,128,1024]{2,1,0:T(8,128)(2,1)S(1)} %pad_maximum_fusion.13.refs_4_), channel_id=1, source_target_pairs={{0,8},{4,12},{8,0},{12,4},{16,24},{20,28},{24,16},{28,20},{1,9},{5... | collective-permute-start | bytes 1572872 | tf_op jit(solution)/shard_map/ppermute | solution.py:51
  506.9 37.1 %collective-permute-start.119 = (bf16[2,128,1024]{2,1,0:T(8,128)(2,1)S(1)}, bf16[2,128,1024]{2,1,0:T(8,128)(2,1)}, u32[]{:S(2)}, u32[]{:S(2)}) collective-permute-start(bf16[2,128,1024]{2,1,0:T(8,128)(2,1)S(1)} %pad_maximum_fusion.12.refs_0_), channel_id=1, source_target_pairs={{0,16},{4,20},{8,24},{12,28},{16,0},{20,4},{24,8},{28,12},{1,17},{... | collective-permute-start | bytes 1572872 | tf_op jit(solution)/shard_map/ppermute | solution.py:51
  507.2 53.2 %all-to-all-start.2 = ((bf16[1,2,8,32,1024]{4,3,1,0,2:T(8,128)(2,1)}), bf16[1,2,8,32,1024]{4,3,1,0,2:T(8,128)(2,1)S(1)}, u32[]{:S(2)}, u32[]{:S(2)}) async-start(bf16[1,2,8,32,1024]{4,3,1,0,2:T(8,128)(2,1)} %pad_maximum_fusion.2), calls=%async_computation.2 | async-start | bytes 2097152 | tf_op jit(solution)/shard_map/all_to_all | solution.py:622
  542.8 35.3 %collective-permute-start.139 = (bf16[2,128,1024]{2,1,0:T(8,128)(2,1)S(1)}, bf16[2,128,1024]{2,1,0:T(8,128)(2,1)}, u32[]{:S(2)}, u32[]{:S(2)}) collective-permute-start(bf16[2,128,1024]{2,1,0:T(8,128)(2,1)S(1)} %pad_maximum_fusion.13.refs_4_), channel_id=1, source_target_pairs={{0,4},{4,0},{8,12},{12,8},{16,20},{20,16},{24,28},{28,24},{1,5},{5... | collective-permute-start | bytes 1572872 | tf_op jit(solution)/shard_map/ppermute | solution.py:51
  543.5 34.6 %collective-permute-start.120 = (bf16[2,128,1024]{2,1,0:T(8,128)(2,1)S(1)}, bf16[2,128,1024]{2,1,0:T(8,128)(2,1)}, u32[]{:S(2)}, u32[]{:S(2)}) collective-permute-start(bf16[2,128,1024]{2,1,0:T(8,128)(2,1)S(1)} %pad_maximum_fusion.12.refs_0_), channel_id=1, source_target_pairs={{0,4},{4,0},{8,12},{12,8},{16,20},{20,16},{24,28},{28,24},{1,5},{5... | collective-permute-start | bytes 1572872 | tf_op jit(solution)/shard_map/ppermute | solution.py:51
  544.0 34.1 %collective-permute-start.140 = (bf16[2,128,1024]{2,1,0:T(8,128)(2,1)}, bf16[2,128,1024]{2,1,0:T(8,128)(2,1)}, u32[]{:S(2)}, u32[]{:S(2)}) collective-permute-start(bf16[2,128,1024]{2,1,0:T(8,128)(2,1)} %collective-permute-done.138.refs_5_), channel_id=1, source_target_pairs={{0,4},{4,0},{8,12},{12,8},{16,20},{20,16},{24,28},{28,24},{1,5},{5... | collective-permute-start | bytes 1572872 | tf_op jit(solution)/shard_map/ppermute | solution.py:51
  544.0 34.1 %collective-permute-start.121 = (bf16[2,128,1024]{2,1,0:T(8,128)(2,1)}, bf16[2,128,1024]{2,1,0:T(8,128)(2,1)}, u32[]{:S(2)}, u32[]{:S(2)}) collective-permute-start(bf16[2,128,1024]{2,1,0:T(8,128)(2,1)} %collective-permute-done.119.refs_1_), channel_id=1, source_target_pairs={{0,4},{4,0},{8,12},{12,8},{16,20},{20,16},{24,28},{28,24},{1,5},{5... | collective-permute-start | bytes 1572872 | tf_op jit(solution)/shard_map/ppermute | solution.py:51
  546.1 28.1 %collective-permute-start.83 = (bf16[2,2,128,256]{3,2,1,0:T(8,128)(2,1)}, bf16[2,2,128,256]{3,2,1,0:T(8,128)(2,1)}, u32[]{:S(2)}, u32[]{:S(2)}) collective-permute-start(bf16[2,2,128,256]{3,2,1,0:T(8,128)(2,1)} %collective-permute-done.81.refs_1_), channel_id=1, source_target_pairs={{0,4},{4,0},{8,12},{12,8},{16,20},{20,16},{24,28},{28,24},{1,5},{5... | collective-permute-start | bytes 786440 | tf_op jit(solution)/shard_map/ppermute | solution.py:51
  (238 other events, 2509.1 us)

commit v2 on v1

v2 whole, which is shorter than its diff:
```python
import functools

import jax
import jax.numpy as jnp
from jax import lax
from jax.experimental import pallas as pl
from jax.experimental.pallas import tpu as pltpu
from jax.sharding import PartitionSpec as P

HEAD = 64
LANES = 128
EPSILON = 1e-06
NEGATIVE = -1e30
ROOT = 0.7978845608028654
CUBE = 0.044715
SCALE = HEAD**-0.5
F32 = jnp.float32
BF16 = jnp.bfloat16
VMEM_BYTES = 36 * 1024 * 1024

NN = (((1,), (0,)), ((), ()))
NT = (((1,), (1,)), ((), ()))
TN = (((0,), (0,)), ((), ()))

IN_HBM = pl.BlockSpec(memory_space=pltpu.HBM)
IN_VMEM = pl.BlockSpec(memory_space=pltpu.VMEM)
IN_SMEM = pl.BlockSpec(memory_space=pltpu.SMEM)


def mm(left, right, dims):
    return lax.dot_general(left, right, dims, preferred_element_type=F32)


def cost(flops, bytes_accessed, transcendentals=0):
    return pl.CostEstimate(
        flops=int(flops), bytes_accessed=int(bytes_accessed), transcendentals=int(transcendentals)
    )


def params(semantics=None):
    return pltpu.CompilerParams(dimension_semantics=semantics, vmem_limit_bytes=VMEM_BYTES)


def combos(bits):
    found = [0]
    for bit in bits:
        found = [i | extra for i in found for extra in (0, 1 << bit)]
    return found


def exchange_plan(chips, shared):
    bits = list(range(chips.bit_length() - 1))
    if not shared:
        return ((bits, []), (bits[::-1], []))
    cut = len(bits) // 2
    return ((bits[:cut], bits[cut:]), (bits[cut:], bits[:cut]))


def exchange(value, offset):
    ranks = lax.axis_size("seq")
    return lax.ppermute(value, "seq", [(i, i ^ offset) for i in range(ranks)])


def across(value, bit):
    return exchange(value, 2 << bit)


def other_core(value):
    return exchange(value, 1)


def ring(value):
    depth = lax.axis_size("mp")
    cycle = [0] + list(range(1, depth, 2)) + list(range(2, depth, 2))[::-1]
    pairs = [(cycle[i], cycle[(i + 1) % depth]) for i in range(depth)]
    return lax.ppermute(value, "mp", pairs)


def joined(arrays):
    return arrays[0] if len(arrays) == 1 else jnp.concatenate(arrays, axis=0)


def gather_places(plan):
    bits, kept = plan
    held = [combos(kept)]
    for bit in bits:
        flat = [i for part in held for i in part]
        held = [flat, [i | (1 << bit) for i in flat]]
    return held


def scatter_order(plan):
    return combos(plan[0] + plan[1])


def added(left, right):
    return (left.astype(F32) + right.astype(F32)).astype(BF16)


def swapped(value, at, count):
    shape = value.shape
    parts = value.reshape((2**at, 2, 2 ** (count - at - 1)) + shape[1:])
    return jnp.concatenate([parts[:, 1:], parts[:, :1]], axis=1).reshape(shape)


class Pipe:
    def __init__(self):
        self.slot = 0
        self.flights = []

    def launch(self, chain):
        self.advance(chain, None)

    def advance(self, chain, got):
        try:
            arrays, slots = chain.send(got)
        except StopIteration:
            return
        self.flights.append((chain, arrays, self.slot + slots))

    def step(self, outs):
        self.slot += 1
        due = [f for f in self.flights if f[2] <= self.slot]
        self.flights = [f for f in self.flights if f[2] > self.slot]
        outs, got = lax.optimization_barrier((outs, [f[1] for f in due]))
        for flight, arrays in zip(due, got):
            self.advance(flight[0], arrays)
        return outs

    def drain(self):
        while self.flights:
            due, self.flights = self.flights, []
            self.slot = max(self.slot, min(f[2] for f in due))
            for flight in due:
                self.advance(flight[0], flight[1])


def gather_chain(pieces, plans, done):
    held = [[part] for part in pieces]
    for at in range(max(len(plan[0]) for plan in plans)):
        whole = [joined(parts) for parts in held]
        got = yield [across(w, plan[0][at]) for w, plan in zip(whole, plans)], 1
        held = [[w, g] for w, g in zip(whole, got)]
    done(held[0] + held[1])


def weights_chain(pipe, pieces, split, plans, count, done):
    for k in range(1, count):
        pieces = yield [ring(part) for part in pieces], 1
        pipe.launch(gather_chain(split(pieces), plans, functools.partial(done, k)))


def scatter_chain(parts, plans, done):
    lows, highs = parts[::2], parts[1::2]
    steps = max(len(plan[0]) for plan in plans)
    for at in range(steps):
        got = yield [across(part, plan[0][at]) for part, plan in zip(highs, plans)], 1
        if at + 1 < steps:
            half = lows[0].shape[0] // 2
            highs = [added(t[half:], g[half:]) for t, g in zip(lows, got)]
            lows = [added(t[:half], g[:half]) for t, g in zip(lows, got)]
        else:
            lows = [added(t, g) for t, g in zip(lows, got)]
    done(lows)


class Collect:
    def __init__(self, pipe, count, plans, done):
        self.pipe, self.count, self.plans, self.done = pipe, count, plans, done
        self.parts, self.next, self.sums, self.busy = {}, 1 % count, None, False

    def ready(self, k, totals):
        self.parts[k] = totals
        self.go()

    def go(self):
        if self.busy or self.next is None or self.next not in self.parts:
            return
        part = joined(self.parts[self.next])
        self.sums = part if self.sums is None else added(self.sums, part)
        if self.next == 0:
            self.next = None
            half = self.sums.shape[0] // 2
            self.pipe.launch(self.spread([self.sums[:half], self.sums[half:]]))
            return
        self.next = (self.next + 1) % self.count
        self.busy = True
        self.pipe.launch(self.hop())

    def hop(self):
        (self.sums,) = yield [ring(self.sums)], 1
        self.busy = False
        self.go()

    def spread(self, totals):
        counts = [len(plan[1]) for plan in self.plans]
        for at in range(max(counts)):
            got = yield [across(t, plan[1][at]) for t, plan in zip(totals, self.plans)], 1
            totals = [added(t, swapped(g, at, n)) for t, g, n in zip(totals, got, counts)]
        self.pipe.launch(gather_chain(totals, self.plans, self.cores))

    def cores(self, held):
        def chain():
            got = yield [other_core(part) for part in held], 1
            self.done(held + got)

        self.pipe.launch(chain())


def sum_everywhere(value):
    for axis in ("seq", "mp"):
        size = lax.axis_size(axis)
        step = 1
        while step < size:
            value = value + lax.ppermute(value, axis, [(i, i ^ step) for i in range(size)])
            step *= 2
    return value


def select_kernel(place_ref, base_ref, out_ref):
    span = base_ref.shape[1]
    for at in range(base_ref.shape[0]):
        place = place_ref[at]
        hot = lax.broadcasted_iota(jnp.int32, (place.shape[0], span), 1) == place
        out_ref[at] = mm(hot.astype(BF16), base_ref[at], NN).astype(BF16)


def together(group, span):
    size = max(1, min(group, 1024 // span))
    while group % size:
        size -= 1
    return size


def select_rows(place, base):
    group, span, width = base.shape
    slots = place.shape[1]
    size = together(group, span)
    return pl.pallas_call(
        select_kernel,
        grid=(group // size,),
        in_specs=[
            pl.BlockSpec((size, slots, 1), lambda g: (g, 0, 0)),
            pl.BlockSpec((size, span, width), lambda g: (g, 0, 0)),
        ],
        out_specs=pl.BlockSpec((size, slots, width), lambda g: (g, 0, 0)),
        out_shape=jax.ShapeDtypeStruct((group, slots, width), BF16),
        compiler_params=params(("arbitrary",)),
        cost_estimate=cost(2 * group * slots * span * width, 2 * group * (span + slots) * width),
    )(place[:, :, None], base)


def add_kernel(place_ref, base_ref, rows_ref, out_ref):
    span = base_ref.shape[1]
    for at in range(base_ref.shape[0]):
        place = place_ref[at]
        hot = lax.broadcasted_iota(jnp.int32, (span, place.shape[1]), 0) == place
        moved = mm(hot.astype(BF16), rows_ref[at], NN)
        out_ref[at] = (base_ref[at].astype(F32) + moved).astype(BF16)


def add_rows(place, base, rows):
    group, span, width = base.shape
    slots = place.shape[1]
    size = together(group, span)
    block = pl.BlockSpec((size, span, width), lambda g: (g, 0, 0))
    return pl.pallas_call(
        add_kernel,
        grid=(group // size,),
        in_specs=[
            pl.BlockSpec((size, 1, slots), lambda g: (g, 0, 0)),
            block,
            pl.BlockSpec((size, slots, width), lambda g: (g, 0, 0)),
        ],
        out_specs=block,
        out_shape=jax.ShapeDtypeStruct(base.shape, BF16),
        compiler_params=params(("arbitrary",)),
        cost_estimate=cost(2 * group * slots * span * width, 4 * group * span * width),
    )(place[:, None, :], base, rows)


def start_all(copies, sems):
    started = []
    for at, (source, target) in enumerate(copies):
        copy = pltpu.make_async_copy(source, target, sems.at[at])
        copy.start()
        started.append(copy)
    return started


def attention_copies(chip, sources, places, target):
    if len(sources) == 1:
        return [(sources[0], target)]
    half = len(sources) // 2
    depth = sources[0].shape[2]
    copies = []
    for side in range(2):
        for source, ids in zip(sources[side * half : (side + 1) * half], places[side]):
            for at, index in enumerate(ids):
                start = pl.multiple_of((chip ^ index) * depth, depth)
                copies.append(
                    (
                        source.at[at],
                        target.at[pl.ds(2 * side, 2), pl.ds(start, depth), :],
                    )
                )
    return copies


def mlp_copies(chip, sources, places, order, targets):
    half = len(sources) // 2
    copies = []
    for place, index in enumerate(order):
        for side in range(2):
            target = targets[side]
            if half == 1:
                depth = target.shape[0] // len(order)
                start = pl.multiple_of((chip ^ index) * depth, depth)
                source = sources[side].at[pl.ds(start, depth), :]
            else:
                for array, ids in zip(sources[side * half : (side + 1) * half], places[side]):
                    if index in ids:
                        source = array.at[ids.index(index)]
                        depth = array.shape[1]
            copies.append((source, target.at[pl.ds(place * depth, depth), :]))
    return copies


def row_blocks(rows):
    blocks = []
    for start in (0, rows // 2):
        half = rows // 6
        for first, last, low, high in ((0, 1, 0, 1), (1, 2, 0, 2), (2, 3, 2, 3)):
            blocks.append(tuple(start + half * at for at in (first, last, low, high)))
    return blocks


def causal(first, last, low, high):
    shape = (last - first, high - low)
    row = lax.broadcasted_iota(jnp.int32, shape, 0) + (first - low)
    return row >= lax.broadcasted_iota(jnp.int32, shape, 1)


def head_groups(columns):
    lanes = min(LANES, columns)
    return [
        (slice(at, at + lanes), at // HEAD, lanes // HEAD) for at in range(0, columns, lanes)
    ]


def own_lanes(value, side, heads):
    if heads == 1:
        return value
    lane = lax.broadcasted_iota(jnp.int32, (1, value.shape[1]), 1)
    mine = (lane >= HEAD) if side else (lane < HEAD)
    return jnp.where(mine, value, jnp.zeros_like(value))


def finish(total, last, outs):
    if not last:
        outs[0][...] = total
        return
    half = total.shape[0] // 2
    outs[0][...] = total[:half]
    outs[1][...] = total[half:].astype(BF16)


def sum_shapes(rows, width, last):
    if not last:
        return [jax.ShapeDtypeStruct((rows, width), F32)]
    return [
        jax.ShapeDtypeStruct((rows // 2, width), F32),
        jax.ShapeDtypeStruct((rows // 2, width), BF16),
    ]


def attention_forward_kernel(places, n_sources, has_acc, last, chip_ref, normed_ref, *refs):
    sources, refs = refs[:n_sources], refs[n_sources:]
    if has_acc:
        acc_ref, refs = refs[0], refs[1:]
    sums, refs = refs[: 1 + last], refs[1 + last :]
    heads_ref, mixed_ref, log_ref, held, sems = refs
    for copy in start_all(attention_copies(chip_ref[0], sources, places, held), sems):
        copy.wait()
    rows = normed_ref.shape[0]
    for c in range(3):
        heads_ref[c] = mm(normed_ref[...], held[c], NN).astype(BF16)
    lane = lax.broadcasted_iota(jnp.int32, (1, LANES), 1)
    for first, end, low, high in row_blocks(rows):
        seen = causal(first, end, low, high)
        logs = jnp.zeros((end - first, LANES), F32)
        for lanes, head, heads in head_groups(held.shape[2]):
            query = heads_ref[0, first:end, lanes]
            keys = heads_ref[1, low:high, lanes]
            values = heads_ref[2, low:high, lanes]
            out = None
            for side in range(heads):
                scores = mm(own_lanes(query, side, heads), keys, NT) * SCALE
                scores = jnp.where(seen, scores, NEGATIVE)
                peak = jnp.max(scores, axis=-1, keepdims=True)
                raised = jnp.exp(scores - peak)
                total = jnp.sum(raised, axis=-1, keepdims=True)
                weights = (raised * (1.0 / total)).astype(BF16)
                part = own_lanes(mm(weights, values, NN), side, heads)
                out = part if out is None else out + part
                logs = jnp.where(lane == head + side, peak + jnp.log(total), logs)
            mixed_ref[first:end, lanes] = out.astype(BF16)
        log_ref[first:end, :] = logs
    attended = mm(mixed_ref[...], held[3], NT)
    if has_acc:
        attended = attended + acc_ref[...]
    finish(attended, last, sums)


def attention_forward(chip, normed, sources, places, acc, last):
    rows, width = normed.shape
    columns = sources[0].shape[-1]
    has_acc = acc is not None
    n_sources = len(sources)
    n_copies = 1 if n_sources == 1 else lax.axis_size("seq")
    flops = 2 * rows * width * columns * 4 + rows * rows * columns
    return pl.pallas_call(
        functools.partial(attention_forward_kernel, places, n_sources, has_acc, last),
        in_specs=[IN_SMEM, IN_VMEM] + [IN_HBM] * n_sources + [IN_VMEM] * has_acc,
        out_specs=[IN_VMEM] * (4 + last),
        out_shape=sum_shapes(rows, width, last)
        + [
            jax.ShapeDtypeStruct((3, rows, columns), BF16),
            jax.ShapeDtypeStruct((rows, columns), BF16),
            jax.ShapeDtypeStruct((rows, LANES), F32),
        ],
        scratch_shapes=[
            pltpu.VMEM((4, width, columns), BF16),
            pltpu.SemaphoreType.DMA((n_copies,)),
        ],
        input_output_aliases={2 + n_sources: 0} if has_acc and not last else {},
        compiler_params=params(),
        cost_estimate=cost(flops, 8 * rows * width + 8 * width * columns, rows * rows * 2),
    )(chip, normed, *sources, *([acc] if has_acc else []))


def attention_backward_kernel(
    places,
    orders,
    n_sources,
    has_acc,
    last,
    chip_ref,
    grad_ref,
    normed_ref,
    heads_ref,
    mixed_ref,
    log_ref,
    *refs,
):
    sources, refs = refs[:n_sources], refs[n_sources:]
    if has_acc:
        acc_ref, refs = refs[0], refs[1:]
    sums, refs = refs[: 1 + last], refs[1 + last :]
    outs, refs = refs[:4], refs[4:]
    held, grad_held, grad_heads, sems, out_sems = refs
    chip = chip_ref[0]
    copies = start_all(attention_copies(chip, sources, places, held), sems)
    rows = normed_ref.shape[0]
    width = held.shape[2]
    depth = outs[0].shape[2]
    grad_held[3] = mm(grad_ref[...], mixed_ref[...], TN).astype(BF16)
    for copy in copies:
        copy.wait()
    grad_mixed = mm(grad_ref[...], held[3], NN).astype(BF16)
    lane = lax.broadcasted_iota(jnp.int32, (1, LANES), 1)
    for lanes, head, heads in head_groups(width):
        key_parts, value_parts = [], []
        for first, end, low, high in row_blocks(rows):
            query = heads_ref[0, first:end, lanes]
            keys = heads_ref[1, low:high, lanes]
            values = heads_ref[2, low:high, lanes]
            grad_out = grad_mixed[first:end, lanes]
            logs = log_ref[first:end, :]
            seen = causal(first, end, low, high)
            grad_query = grad_keys = grad_values = None
            for side in range(heads):
                own_query = own_lanes(query, side, heads)
                own_grad = own_lanes(grad_out, side, heads)
                log_total = jnp.sum(
                    jnp.where(lane == head + side, logs, 0.0), axis=-1, keepdims=True
                )
                scores = jnp.where(seen, mm(own_query, keys, NT) * SCALE, NEGATIVE)
                shares = jnp.exp(scores - log_total)
                grad_weights = mm(own_grad, values, NT)
                inner = jnp.sum(shares * grad_weights, axis=-1, keepdims=True)
                grad_scores = (shares * (grad_weights - inner)).astype(BF16)
                weights = shares.astype(BF16)
                part_query = own_lanes(mm(grad_scores, keys, NN), side, heads)
                part_keys = mm(grad_scores, own_query, TN)
                part_values = mm(weights, own_grad, TN)
                if side == 0:
                    grad_query, grad_keys, grad_values = part_query, part_keys, part_values
                else:
                    grad_query = grad_query + part_query
                    grad_keys = grad_keys + part_keys
                    grad_values = grad_values + part_values
            grad_heads[0, first:end, lanes] = (grad_query * SCALE).astype(BF16)
            key_parts.append(grad_keys)
            value_parts.append(grad_values)
        half = rows // 6
        for c, parts, scale in ((1, key_parts, SCALE), (2, value_parts, 1.0)):
            for pair in range(2):
                one, two, three = parts[3 * pair : 3 * pair + 3]
                for at, value in enumerate((one + two[:half], two[half:], three)):
                    start = (3 * pair + at) * half
                    grad_heads[c, start : start + half, lanes] = (value * scale).astype(BF16)
    copies = []
    for side, pieces in ((1, (2, 3)), (0, (0, 1))):
        for c in pieces:
            if c < 3:
                grad_held[c] = mm(normed_ref[...], grad_heads[c], TN).astype(BF16)
        for at, index in enumerate(orders[side]):
            start = pl.multiple_of((chip ^ index) * depth, depth)
            high, at = divmod(at, len(orders[side]) // 2)
            copy = pltpu.make_async_copy(
                grad_held.at[pl.ds(2 * side, 2), pl.ds(start, depth), :],
                outs[2 * side + high].at[at],
                out_sems.at[len(copies)],
            )
            copy.start()
            copies.append(copy)
    grad_normed = mm(grad_heads[0], held[0], NT)
    for c in range(1, 3):
        grad_normed = grad_normed + mm(grad_heads[c], held[c], NT)
    if has_acc:
        grad_normed = grad_normed + acc_ref[...]
    finish(grad_normed, last, sums)
    for copy in copies:
        copy.wait()


def attention_backward(chip, grad, normed, saved, sources, places, orders, acc, last):
    rows, width = normed.shape
    columns = sources[0].shape[-1]
    chips = lax.axis_size("seq") // 2
    has_acc = acc is not None
    n_sources = len(sources)
    n_copies = 1 if n_sources == 1 else 2 * chips
    piece = jax.ShapeDtypeStruct((chips // 2, 2, width // chips, columns), BF16)
    flops = 2 * rows * width * columns * 8 + 3 * rows * rows * columns
    return pl.pallas_call(
        functools.partial(
            attention_backward_kernel, places, orders, n_sources, has_acc, last
        ),
        in_specs=[IN_SMEM] + [IN_VMEM] * 5 + [IN_HBM] * n_sources + [IN_VMEM] * has_acc,
        out_specs=[IN_VMEM] * (1 + last) + [IN_HBM] * 4,
        out_shape=sum_shapes(rows, width, last) + [piece] * 4,
        scratch_shapes=[
            pltpu.VMEM((4, width, columns), BF16),
            pltpu.VMEM((4, width, columns), BF16),
            pltpu.VMEM((3, rows, columns), BF16),
            pltpu.SemaphoreType.DMA((n_copies,)),
            pltpu.SemaphoreType.DMA((2 * chips,)),
        ],
        input_output_aliases={6 + n_sources: 0} if has_acc and not last else {},
        compiler_params=params(),
        cost_estimate=cost(flops, 12 * rows * width + 16 * width * columns, rows * rows * 2),
    )(chip, grad, normed, *saved, *sources, *([acc] if has_acc else []))


def mlp_kernel(places, order, orders, n_sources, has_acc, last, chip_ref, normed_ref, grad_ref, *refs):
    sources, refs = refs[:n_sources], refs[n_sources:]
    if has_acc:
        acc_in, refs = refs[:2], refs[2:]
    sums, refs = refs[: 2 + 2 * last], refs[2 + 2 * last :]
    outs, refs = refs[:4], refs[4:]
    up_held, down_held, up_grad, down_grad, active_held, upward_held, sems, out_sems = refs
    copies = start_all(mlp_copies(chip_ref[0], sources, places, order, (up_held, down_held)), sems)
    hidden = up_held.shape[0]
    depth = hidden // len(order)
    step = max(depth, min(256, hidden))
    waited = 0
    leaving = []
    for start in range(0, hidden, step):
        ready = 2 * ((start + step) // depth)
        for copy in copies[waited:ready]:
            copy.wait()
        waited = ready
        chunk = slice(start, start + step)
        upward = mm(normed_ref[...], up_held[chunk], NT)
        square = upward * upward
        bent = jnp.tanh(ROOT * upward * (1.0 + CUBE * square))
        active = (0.5 * upward * (1.0 + bent)).astype(BF16)
        slope = 0.5 * (1.0 + bent) + 0.5 * ROOT * upward * (1.0 - bent * bent) * (
            1.0 + 3.0 * CUBE * square
        )
        grad_active = mm(grad_ref[...], down_held[chunk], NT)
        grad_upward = (grad_active * slope).astype(BF16)
        active_held[:, chunk] = active
        upward_held[:, chunk] = grad_upward
        up_grad[chunk] = mm(grad_upward, normed_ref[...], TN).astype(BF16)
        down_grad[chunk] = mm(active, grad_ref[...], TN).astype(BF16)
        for at in range(start // depth, (start + step) // depth):
            for side, grads in enumerate((up_grad, down_grad)):
                place = orders[side].index(order[at])
                high, place = divmod(place, len(order) // 2)
                copy = pltpu.make_async_copy(
                    grads.at[pl.ds(at * depth, depth), :],
                    outs[2 * side + high].at[place],
                    out_sems.at[2 * at + side],
                )
                copy.start()
                leaving.append(copy)
    for i, (left, right) in enumerate(((active_held, down_held), (upward_held, up_held))):
        total = mm(left[...], right[...], NN)
        if has_acc:
            total = total + acc_in[i][...]
        finish(total, last, sums[i * (1 + last) : (i + 1) * (1 + last)])
    for copy in leaving:
        copy.wait()


def mlp(chip, normed, grad, sources, hidden, places, order, orders, acc, last):
    rows, width = normed.shape
    chips = len(order)
    depth = hidden // chips
    has_acc = acc is not None
    n_sources = len(sources)
    piece = jax.ShapeDtypeStruct((chips // 2, depth, width), BF16)
    aliased = {3 + n_sources: 0, 4 + n_sources: 1} if has_acc and not last else {}
    return pl.pallas_call(
        functools.partial(mlp_kernel, places, order, orders, n_sources, has_acc, last),
        in_specs=[IN_SMEM] + [IN_VMEM] * 2 + [IN_HBM] * n_sources + [IN_VMEM] * (2 * has_acc),
        out_specs=[IN_VMEM] * (2 + 2 * last) + [IN_HBM] * 4,
        out_shape=sum_shapes(rows, width, last) * 2 + [piece] * 4,
        scratch_shapes=[pltpu.VMEM((hidden, width), BF16)] * 4
        + [pltpu.VMEM((rows, hidden), BF16)] * 2
        + [
            pltpu.SemaphoreType.DMA((2 * chips,)),
            pltpu.SemaphoreType.DMA((2 * chips,)),
        ],
        input_output_aliases=aliased,
        compiler_params=params(),
        cost_estimate=cost(
            12 * rows * width * hidden, 20 * rows * width + 8 * width * hidden, rows * hidden
        ),
    )(chip, normed, grad, *sources, *(acc if has_acc else []))


def place_attention_kernel(places, n_sources, chip_ref, core_ref, *refs):
    sources, refs = refs[:n_sources], refs[n_sources:]
    qkv_ref, out_ref, held, sems = refs
    half = n_sources // 2
    copies = []
    for which, core in enumerate((core_ref[0], 1 - core_ref[0])):
        copies += attention_copies(
            chip_ref[0], sources[which * half : (which + 1) * half], places, held.at[core]
        )
    for copy in start_all(copies, sems):
        copy.wait()
    columns = held.shape[3]
    for c in range(3):
        qkv_ref[c] = jnp.concatenate([held[0, c], held[1, c]], axis=-1).astype(F32)
    for core in range(2):
        out_ref[core * columns : (core + 1) * columns, :] = held[core, 3].astype(F32).T


def place_attention(chip, core, sources, places, width):
    columns = sources[0].shape[-1]
    n_sources = len(sources)
    return pl.pallas_call(
        functools.partial(place_attention_kernel, places, n_sources),
        in_specs=[IN_SMEM, IN_SMEM] + [IN_HBM] * n_sources,
        out_specs=[IN_VMEM] * 2,
        out_shape=[
            jax.ShapeDtypeStruct((3, width, 2 * columns), F32),
            jax.ShapeDtypeStruct((2 * columns, width), F32),
        ],
        scratch_shapes=[
            pltpu.VMEM((2, 4, width, columns), BF16),
            pltpu.SemaphoreType.DMA((2 * lax.axis_size("seq"),)),
        ],
        compiler_params=params(),
        cost_estimate=cost(0, 48 * width * columns),
    )(chip, core, *sources)


def place_mlp_kernel(places, order, n_sources, chip_ref, core_ref, *refs):
    sources, refs = refs[:n_sources], refs[n_sources:]
    out_ref, up_held, down_held, out_held, sems, out_sems = refs
    chip, core = chip_ref[0], core_ref[0]
    hidden, width = up_held.shape[1:]
    half = n_sources // 2
    copies = []
    for which in range(2):
        targets = (up_held.at[which], down_held.at[which])
        copies += mlp_copies(
            chip, sources[which * half : (which + 1) * half], places, order, targets
        )
    copies = start_all(copies, sems)
    depth = hidden // len(order)
    tiles = width // LANES
    size = depth * 2 * tiles
    moved = []
    for which in range(2):
        for at, index in enumerate(order):
            base = len(moved)
            for side, part in enumerate((up_held, down_held)):
                copies[2 * base + side].wait()
                rows = part[which, at * depth : (at + 1) * depth, :].astype(F32)
                for tile in range(tiles):
                    out_held[pl.ds(base * size + 2 * tile + side, depth, stride=2 * tiles), :] = (
                        rows[:, tile * LANES : (tile + 1) * LANES]
                    )
            block = ((core if which == 0 else 1 - core) * len(order) + (chip ^ index)) * size
            copy = pltpu.make_async_copy(
                out_held.at[pl.ds(base * size, size), :],
                out_ref.at[pl.ds(pl.multiple_of(block, size), size), :],
                out_sems.at[base],
            )
            copy.start()
            moved.append(copy)
    for copy in moved:
        copy.wait()


def place_mlp(chip, core, sources, places, order, hidden):
    width = sources[0].shape[-1]
    n_sources = len(sources)
    tiles = width // LANES
    chips = len(order)
    rows = pl.pallas_call(
        functools.partial(place_mlp_kernel, places, order, n_sources),
        in_specs=[IN_SMEM, IN_SMEM] + [IN_HBM] * n_sources,
        out_specs=IN_HBM,
        out_shape=jax.ShapeDtypeStruct((hidden * 2 * tiles, LANES), F32),
        scratch_shapes=[
            pltpu.VMEM((2, hidden // 2, width), BF16),
            pltpu.VMEM((2, hidden // 2, width), BF16),
            pltpu.VMEM((hidden * 2 * tiles, LANES), F32),
            pltpu.SemaphoreType.DMA((4 * chips,)),
            pltpu.SemaphoreType.DMA((2 * chips,)),
        ],
        compiler_params=params(),
        cost_estimate=cost(0, 12 * hidden * width),
    )(chip, core, *sources)
    shaped = rows.reshape(hidden, tiles, 2, LANES)
    return shaped.transpose(0, 2, 1, 3).reshape(hidden, 2, width)


def rms_scale(values):
    return lax.rsqrt(jnp.mean(values * values, axis=-1, keepdims=True) + EPSILON)


def norm_back(grad_normed, unit_rows, scale, gain):
    scaled = gain * grad_normed
    return scale * (scaled - unit_rows * jnp.mean(unit_rows * scaled, axis=-1, keepdims=True))


def pack(first_longer, got):
    ranks, held, slots, width = got.shape
    longer = jnp.where(first_longer, got[:, 0], got[:, 1])
    shorter = jnp.where(first_longer, got[: ranks // 2, 1], got[: ranks // 2, 0])
    return jnp.concatenate(
        [longer.reshape(ranks * slots, width), shorter.reshape(ranks * slots // 2, width)]
    )


def unpack(first_longer, packed, ranks):
    rows, width = packed.shape
    half = rows // 3
    longer = packed[: 2 * half]
    shorter = jnp.concatenate([packed[2 * half :], jnp.zeros((half, width), packed.dtype)])
    both = jnp.stack(
        [
            jnp.where(first_longer, longer, shorter),
            jnp.where(first_longer, shorter, longer),
        ]
    )
    return both.reshape(1, 2, ranks, 2 * half // ranks, width)


def on_device(tokens, cotangent, lengths, routed, gain_attn, gain_mlp, router, w_qkv, w_out, w_mlp):
    group, span, width = tokens.shape
    slots = routed.shape[1]
    ranks = lax.axis_size("seq")
    count = lax.axis_size("mp")
    held = group // ranks
    chips = ranks // 2
    columns = w_qkv.shape[2] // 2
    hidden = w_mlp.shape[0] // 2
    me = lax.axis_index("seq").astype(jnp.int32)
    chip, core = me // 2, me % 2
    chip_array, core_array = chip[None], core[None]
    whole_plans, shared_plans = exchange_plan(chips, False), exchange_plan(chips, True)
    places = [gather_places(plan) for plan in whole_plans]
    orders = [scatter_order(plan) for plan in whole_plans]
    shared_places = [gather_places(plan) for plan in shared_plans]
    shared_orders = [scatter_order(plan) for plan in shared_plans]
    order = orders[0]
    pipe = Pipe()

    attn_shards, mlp_shards = {}, {}
    own_attn = jnp.concatenate([w_qkv, w_out.T[None]])
    own_attn = lax.dynamic_slice_in_dim(own_attn, core * columns, columns, 2)
    piece = lax.dynamic_slice_in_dim(own_attn, chip * (width // chips), width // chips, 1)
    attn_shards[0] = [own_attn]
    pipe.launch(
        weights_chain(
            pipe,
            [piece[None]],
            lambda parts: [parts[0][:, :2], parts[0][:, 2:]],
            whole_plans,
            count,
            attn_shards.__setitem__,
        )
    )

    slot = lax.broadcasted_iota(jnp.int32, routed.shape, 1)
    live = me * slots + slot < (lengths // 8)[:, None]
    place = jnp.where(live, slot * 8 + routed % 8, -1)
    pair = lax.dynamic_slice_in_dim(lengths, me * held, held, 0)
    first_longer = pair[0] >= pair[1]
    rows = {}

    def to_holder(value, name):
        value = value.reshape(ranks, held, slots, width)
        got = yield [lax.all_to_all(value, "seq", split_axis=0, concat_axis=0, tiled=True)], 1
        rows[name] = pack(first_longer, got[0]).astype(F32)

    def to_position(value, name):
        value = unpack(first_longer, value, ranks)
        got = yield [lax.all_to_all(value, "seq", split_axis=2, concat_axis=0, tiled=True)], 1
        rows[name] = got[0].reshape(group, slots, width)

    def both_cores(value):
        return jnp.concatenate([value, other_core(value)])

    chosen, cotangent = pipe.step((select_rows(place, tokens), cotangent))
    pipe.launch(to_holder(chosen, "picked"))
    chosen_grad, w_mlp = pipe.step((select_rows(place, cotangent), w_mlp))

    picked = rows["picked"]
    scale_one = rms_scale(picked)
    unit_one = picked * scale_one
    normed_one = both_cores((unit_one * gain_attn).astype(BF16))
    gate = jax.nn.sigmoid(jnp.sum(picked * router, axis=-1, keepdims=True))
    own_mlp = lax.dynamic_slice_in_dim(w_mlp, core * hidden, hidden, 0)
    own_up, own_down = own_mlp[:, 0, :], own_mlp[:, 1, :]
    piece = jnp.stack(
        [
            lax.dynamic_slice_in_dim(part, chip * (hidden // chips), hidden // chips, 0)
            for part in (own_up, own_down)
        ]
    )
    mlp_shards[0] = [own_up, own_down]
    attended, saved = None, []
    for k in range(count):
        while k not in attn_shards:
            normed_one = pipe.step(normed_one)
        out = attention_forward(
            chip_array, normed_one, attn_shards[k], places, attended, k == count - 1
        )
        if k == 0:
            out, piece = pipe.step((out, piece))
            pipe.launch(
                weights_chain(
                    pipe,
                    [piece],
                    lambda parts: [parts[0][:1], parts[0][1:]],
                    whole_plans,
                    count,
                    mlp_shards.__setitem__,
                )
            )
        else:
            out = pipe.step(out)
        if k == max(0, count - 2):
            pipe.launch(to_holder(chosen_grad, "grads"))
        attended, sent, saved_one = out[0], out[-4], out[-3:]
        saved.append(saved_one)
    while "grads" not in rows:
        attended = pipe.step(attended)
    grad_rows = rows["grads"]
    attended = attended + other_core(sent).astype(F32)
    grad_feed = both_cores((gate * grad_rows).astype(BF16))
    middle = picked + attended
    scale_two = rms_scale(middle)
    unit_two = middle * scale_two
    normed_two = both_cores((unit_two * gain_mlp).astype(BF16))

    sums, done = None, {}
    mlp_sums = Collect(pipe, count, whole_plans, functools.partial(done.__setitem__, "mlp"))
    attn_sums = Collect(pipe, count, shared_plans, functools.partial(done.__setitem__, "attn"))
    for k in range(count):
        while k not in mlp_shards:
            normed_two = pipe.step(normed_two)
        out = mlp(
            chip_array,
            normed_two,
            grad_feed,
            mlp_shards[k],
            hidden,
            places,
            order,
            orders,
            sums,
            k == count - 1,
        )
        out = pipe.step(out)
        sums = out[:-4]
        pipe.launch(scatter_chain(out[-4:], whole_plans, functools.partial(mlp_sums.ready, k)))
    grad_normed_two = sums[2] + other_core(sums[3]).astype(F32)
    feed = sums[0] + other_core(sums[1]).astype(F32)
    grad_middle = norm_back(grad_normed_two, unit_two, scale_two, gain_mlp)
    grad_attended = both_cores((gate * grad_rows + grad_middle).astype(BF16))
    delta = attended + feed
    pipe.launch(to_position((gate * delta).astype(BF16), "out"))
    grad_logit = jnp.sum(grad_rows * delta, axis=-1, keepdims=True) * gate * (1.0 - gate)
    router_part = jnp.sum(grad_logit * picked, axis=0)
    mlp_gain_part = jnp.sum(grad_normed_two * unit_two, axis=0)

    grad_sum = None
    for at, k in enumerate(list(range(1, count)) + [0]):
        out = attention_backward(
            chip_array,
            grad_attended,
            normed_one,
            saved[k],
            attn_shards[k],
            places,
            shared_orders,
            grad_sum,
            at == count - 1,
        )
        out = pipe.step(out)
        grad_sum = out[0]
        pipe.launch(scatter_chain(out[-4:], shared_plans, functools.partial(attn_sums.ready, k)))
    grad_normed_one = grad_sum + other_core(out[1]).astype(F32)
    grad_picked = (
        grad_middle
        + norm_back(grad_normed_one, unit_one, scale_one, gain_attn)
        + grad_logit * router
    ).astype(BF16)
    pipe.launch(to_position(grad_picked, "back"))
    attn_gain_part = jnp.sum(grad_normed_one * unit_one, axis=0)
    small = sum_everywhere(jnp.stack([attn_gain_part, mlp_gain_part, router_part]))
    layer_out = pipe.step(add_rows(place, tokens, rows["out"]))
    grad_tokens = pipe.step(add_rows(place, cotangent, rows["back"]))
    while "mlp" not in done:
        grad_tokens = pipe.step(grad_tokens)
    grad_mlp = place_mlp(chip_array, core_array, done["mlp"], places, order, 2 * hidden)
    pipe.drain()
    grad_qkv, grad_out = place_attention(
        chip_array, core_array, done["attn"], shared_places, width
    )
    return (
        layer_out,
        grad_tokens,
        small[0],
        small[1],
        small[2],
        grad_qkv,
        grad_out,
        grad_mlp,
    )


def solution(mesh):
    placed = (
        P("mp", "seq", None),
        P("mp", "seq", None),
        P("mp"),
        P("mp", "seq"),
        P(),
        P(),
        P(),
        P(None, None, "mp"),
        P("mp", None),
        P("mp", None, None),
    )
    return jax.shard_map(
        on_device,
        mesh=mesh,
        in_specs=placed,
        out_specs=(
            P("mp", "seq", None),
            P("mp", "seq", None),
            P(),
            P(),
            P(),
            P(None, None, "mp"),
            P("mp", None),
            P("mp", None, None),
        ),
        check_vma=False,
    )
```

time: 611 us -> 409 us (0.67)
  waiting for transfers between devices: 174 us -> 63.1 us
  Pallas kernels: 179 us -> 130 us
  starting transfers between devices: 142 us -> 108 us
  other arithmetic: 49.9 us -> 42.7 us
    ppermute x112 -> x72, waiting for transfers between devices: 132 us -> 44.2 us  [exchange(): return lax.ppermute(value, 'seq', [(i, i ^ offset) for i in range(ranks)])]
    pallas_call x3 -> x4, Pallas kernels: 41.5 us -> 17 us  [the longest x2 11.1 us: add_rows(): pl.pallas_call(add_kernel, grid=(group // size,), in_specs=[pl.BlockSpec(...]
    ppermute x112 -> x72, starting transfers between devices: 86.8 us -> 65 us  [exchange(): return lax.ppermute(value, 'seq', [(i, i ^ offset) for i in range(ranks)])]
    ppermute x24 -> x12, waiting for transfers between devices: 23.8 us -> 5.54 us  [ring(): return lax.ppermute(value, 'mp', pairs)]
    pallas_call x4, Pallas kernels: 46.3 us -> 29.2 us  [mlp(): pl.pallas_call(functools.partial(mlp_kernel, places, order, orders, n_sou...]
    ppermute x24 -> x12, starting transfers between devices: 32.4 us -> 20.8 us  [ring(): return lax.ppermute(value, 'mp', pairs)]
    convert_element_type x40 -> x31, other arithmetic: 13.5 us -> 19.1 us  [added(): return (left.astype(F32) + right.astype(F32)).astype(BF16)]
    unnamed x256 -> x289, local copies, waits for them, and re-layouts: 39.4 us -> 42.7 us
  transfers between devices with their start and end apart: 145 -> 93, of which waited for: 47 -> 19; matrix products, arithmetic and copies ran while one was open for 11% -> 10% of each run, Pallas kernels for 26% -> 31%
where the time goes in v2:
time: 409 us; the launch traced here: 402 us
  Pallas kernels  130 us (32%)
  starting transfers between devices  108 us (26%)
  waiting for transfers between devices  63.1 us (15%)
  local copies, waits for them, and re-layouts  53.2 us (13%)
  other arithmetic  42.7 us (10%)
  between operations  4.79 us (1%)
    ppermute x72, starting transfers between devices, exchange(): return lax.ppermute(value, 'seq', [(i, i ^ offset) for i in range(ranks)])  65 us
    pallas_call x4, Pallas kernels, attention_backward(): pl.pallas_call(functools.partial(attention_backward_kernel, places, order...  48.8 us
    ppermute x72, waiting for transfers between devices, exchange(): return lax.ppermute(value, 'seq', [(i, i ^ offset) for i in range(ranks)])  44.2 us
    unnamed x289, local copies, waits for them, and re-layouts  42.7 us
    pallas_call x4, Pallas kernels, mlp(): pl.pallas_call(functools.partial(mlp_kernel, places, order, orders, n_sou...  29.2 us
    pallas_call x4, Pallas kernels, attention_forward(): pl.pallas_call(functools.partial(attention_forward_kernel, places, n_sour...  25.9 us
    ppermute x12, starting transfers between devices, ring(): return lax.ppermute(value, 'mp', pairs)  20.8 us
    convert_element_type x31, other arithmetic, added(): return (left.astype(F32) + right.astype(F32)).astype(BF16)  19.1 us
  transfers between devices with their start and end apart: 93, of which 19 were waited for; matrix products, arithmetic and copies ran while one was open for 10% of the time, Pallas kernels for 31%

profile of v2, /device:TPU:0, one launch (start us, length us, event | category | flops | bytes accessed | tf_op | source)
XLA Modules:
  0.0 401.6 jit_solution(12709635940025445967)
XLA Ops:
  6.7 3.4 copy-done
  13.6 3.8 all-to-all-start
  31.2 3.5 collective-permute-done.1
  37.0 3.9 copy.39
  48.7 5.9 %shard_map.163 = (f32[768,1024]{1,0:T(8,128)S(1)}, bf16[3,768,128]{2,1,0:T(8,128)(2,1)S(1)}, bf16[768,128]{1,0:T(8,128)(2,1)S(1)}, f32[768,128]{1,0:T(8,128)S(1)}) custom-call(s32[1]{0:T(128)} %bitcast.1.chip_ref, bf16[768,1024]{1,0:T(8,128)(2,1)S(1)} %pad_maximum_fusion.normed_ref, bf16[4,1024,128]{2,1,0:T(8,128)(2,1)S(1)} %fusion.19.refs_0_), custom_call_target="tpu_custom_call" | custom-call | flops 880803840 | bytes 7340032 | tf_op jit(solution)/shard_map/pallas_call | solution.py:422
  62.2 6.8 %shard_map.164 = (f32[768,1024]{1,0:T(8,128)S(1)}, bf16[3,768,128]{2,1,0:T(8,128)(2,1)S(1)}, bf16[768,128]{1,0:T(8,128)(2,1)S(1)}, f32[768,128]{1,0:T(8,128)S(1)}) custom-call(s32[1]{0:T(128)} %bitcast.1.chip_ref, bf16[768,1024]{1,0:T(8,128)(2,1)S(1)} %pad_maximum_fusion.normed_ref, ...), custom_call_target="tpu_custom_call", output_to_operand_aliasing={{0}: (6, {})} | custom-call | flops 880803840 | bytes 7340032 | tf_op jit(solution)/shard_map/pallas_call | solution.py:422
  79.2 4.3 %all-to-all-start.1 = ((bf16[8,2,32,1024]{3,2,1,0:T(8,128)(2,1)}), bf16[8,2,32,1024]{3,2,1,0:T(8,128)(2,1)}, u32[]{:S(2)}, u32[]{:S(2)}) async-start(bf16[8,2,32,1024]{3,2,1,0:T(8,128)(2,1)} %bitcast.12), calls=%async_computation.1 | async-start | bytes 2097152 | tf_op jit(solution)/shard_map/all_to_all | solution.py:824
  86.3 6.8 %shard_map.165 = (f32[768,1024]{1,0:T(8,128)S(1)}, bf16[3,768,128]{2,1,0:T(8,128)(2,1)S(1)}, bf16[768,128]{1,0:T(8,128)(2,1)S(1)}, f32[768,128]{1,0:T(8,128)S(1)}) custom-call(s32[1]{0:T(128)} %bitcast.1.chip_ref, bf16[768,1024]{1,0:T(8,128)(2,1)S(1)} %pad_maximum_fusion.normed_ref, ...), custom_call_target="tpu_custom_call", output_to_operand_aliasing={{0}: (6, {})} | custom-call | flops 880803840 | bytes 7340032 | tf_op jit(solution)/shard_map/pallas_call | solution.py:422
  107.2 6.5 %shard_map.166 = (f32[384,1024]{1,0:T(8,128)S(1)}, bf16[384,1024]{1,0:T(8,128)(2,1)S(1)}, bf16[3,768,128]{2,1,0:T(8,128)(2,1)S(1)}, bf16[768,128]{1,0:T(8,128)(2,1)S(1)}, f32[768,128]{1,0:T(8,128)S(1)}) custom-call(s32[1]{0:T(128)} %bitcast.1.chip_ref, bf16[768,1024]{1,0:T(8,128)(2,1)S(1)} %pad_maximum_fusion.normed_ref, ...), custom_call_target="tpu_custom_call" | custom-call | flops 880803840 | bytes 7340032 | tf_op jit(solution)/shard_map/pallas_call | solution.py:422
  134.0 7.0 %shard_map.167 = (f32[768,1024]{1,0:T(8,128)S(1)}, f32[768,1024]{1,0:T(8,128)S(1)}, bf16[2,128,1024]{2,1,0:T(8,128)(2,1)S(1)}, bf16[2,128,1024]{2,1,0:T(8,128)(2...) custom-call(s32[1]{0:T(128)} %bitcast.1.chip_ref, ...), custom_call_target="tpu_custom_call" | custom-call | flops 4831838208 | bytes 19922944 | tf_op jit(solution)/shard_map/pallas_call | solution.py:627
  141.0 7.1 %collective-permute-done.30 = bf16[1,128,1024]{2,1,0:T(8,128)(2,1)S(1)} collective-permute-done((bf16[1,128,1024]{2,1,0:T(8,128)(2,1)S(1)}, bf16[1,128,1024]{2,1,0:T(8,128)(2,1)S(1)}, u32[]{:S(2)}, u32[]{:S(2)}) %collective-permute-start.30) | collective-permute-done | bytes 262176 | tf_op jit(solution)/shard_map/ppermute | solution.py:61
  152.4 8.1 %shard_map.168 = (f32[768,1024]{1,0:T(8,128)S(1)}, f32[768,1024]{1,0:T(8,128)S(1)}, bf16[2,128,1024]{2,1,0:T(8,128)(2,1)S(1)}, bf16[2,128,1024]{2,1,0:T(8,128)(2...) custom-call(s32[1]{0:T(128)} %bitcast.1.chip_ref, ...), custom_call_target="tpu_custom_call", output_to_operand_aliasing={{0}: (7, {}), {1}: (8, {})} | custom-call | flops 4831838208 | bytes 19922944 | tf_op jit(solution)/shard_map/pallas_call | solution.py:627
  164.9 8.8 %collective-permute-done.34 = bf16[2,128,1024]{2,1,0:T(8,128)(2,1)S(1)} collective-permute-done((bf16[2,128,1024]{2,1,0:T(8,128)(2,1)S(1)}, bf16[2,128,1024]{2,1,0:T(8,128)(2,1)S(1)}, u32[]{:S(2)}, u32[]{:S(2)}) %collective-permute-start.34) | collective-permute-done | bytes 524320 | tf_op jit(solution)/shard_map/ppermute | solution.py:61
  178.0 7.3 %shard_map.169 = (f32[768,1024]{1,0:T(8,128)S(1)}, f32[768,1024]{1,0:T(8,128)S(1)}, bf16[2,128,1024]{2,1,0:T(8,128)(2,1)S(1)}, bf16[2,128,1024]{2,1,0:T(8,128)(2...) custom-call(s32[1]{0:T(128)} %bitcast.1.chip_ref, ...), custom_call_target="tpu_custom_call", output_to_operand_aliasing={{0}: (7, {}), {1}: (8, {})} | custom-call | flops 4831838208 | bytes 19922944 | tf_op jit(solution)/shard_map/pallas_call | solution.py:627
  187.0 4.1 %collective-permute-done.37 = bf16[1,128,1024]{2,1,0:T(8,128)(2,1)S(1)} collective-permute-done((bf16[1,128,1024]{2,1,0:T(8,128)(2,1)S(1)}, bf16[1,128,1024]{2,1,0:T(8,128)(2,1)S(1)}, u32[]{:S(2)}, u32[]{:S(2)}) %collective-permute-start.37) | collective-permute-done | bytes 262176 | tf_op jit(solution)/shard_map/ppermute | solution.py:61
  197.7 6.8 %shard_map.170 = (f32[384,1024]{1,0:T(8,128)S(1)}, bf16[384,1024]{1,0:T(8,128)(2,1)S(1)}, f32[384,1024]{1,0:T(8,128)S(1)}, bf16[384,1024]{1,0:T(8,128)(2,1)S(1)}...) custom-call(s32[1]{0:T(128)} %bitcast.1.chip_ref, ...), custom_call_target="tpu_custom_call" | custom-call | flops 4831838208 | bytes 19922944 | tf_op jit(solution)/shard_map/pallas_call | solution.py:627
  204.5 4.0 collective-permute-done.41
  215.6 4.4 %all-to-all-start.2 = ((bf16[1,2,8,32,1024]{4,3,1,0,2:T(8,128)(2,1)}), bf16[1,2,8,32,1024]{4,3,1,0,2:T(8,128)(2,1)}, u32[]{:S(2)}, u32[]{:S(2)}) async-start(bf16[1,2,8,32,1024]{4,3,1,0,2:T(8,128)(2,1)} %pad_maximum_fusion.4), calls=%async_computation.2 | async-start | bytes 2097152 | tf_op jit(solution)/shard_map/all_to_all | solution.py:829
  228.0 12.5 %shard_map.171 = (f32[768,1024]{1,0:T(8,128)S(1)}, bf16[2,2,256,128]{3,2,1,0:T(8,128)(2,1)S(1)}, bf16[2,2,256,128]{3,2,1,0:T(8,128)(2,1)S(1)}, bf16[2,2,256,128]...) custom-call(s32[1]{0:T(128)} %bitcast.1.chip_ref, bf16[768,1024]{1,0:T(8,128)(2,1)S(1)} %pad_maximum_fusion.3.grad_ref, ...), custom_call_target="tpu_custom_call" | custom-call | flops 1837105152 | bytes 11534336 | tf_op jit(solution)/shard_map/pallas_call | solution.py:547
  245.0 6.2 %collective-permute-done.48 = bf16[1,128,1024]{2,1,0:T(8,128)(2,1)S(1)} collective-permute-done((bf16[1,128,1024]{2,1,0:T(8,128)(2,1)S(1)}, bf16[1,128,1024]{2,1,0:T(8,128)(2,1)S(1)}, u32[]{:S(2)}, u32[]{:S(2)}) %collective-permute-start.48) | collective-permute-done | bytes 262176 | tf_op jit(solution)/shard_map/ppermute | solution.py:61
  264.3 12.3 %shard_map.173 = (f32[768,1024]{1,0:T(8,128)S(1)}, bf16[2,2,256,128]{3,2,1,0:T(8,128)(2,1)S(1)}, bf16[2,2,256,128]{3,2,1,0:T(8,128)(2,1)S(1)}, bf16[2,2,256,128]...) custom-call(s32[1]{0:T(128)} %bitcast.1.chip_ref, ...), custom_call_target="tpu_custom_call", output_to_operand_aliasing={{0}: (10, {})} | custom-call | flops 1837105152 | bytes 11534336 | tf_op jit(solution)/shard_map/pallas_call | solution.py:547
  286.1 12.4 %shard_map.174 = (f32[768,1024]{1,0:T(8,128)S(1)}, bf16[2,2,256,128]{3,2,1,0:T(8,128)(2,1)S(1)}, bf16[2,2,256,128]{3,2,1,0:T(8,128)(2,1)S(1)}, bf16[2,2,256,128]...) custom-call(s32[1]{0:T(128)} %bitcast.1.chip_ref, ...), custom_call_target="tpu_custom_call", output_to_operand_aliasing={{0}: (10, {})} | custom-call | flops 1837105152 | bytes 11534336 | tf_op jit(solution)/shard_map/pallas_call | solution.py:547
  298.5 4.9 %collective-permute-done.58 = bf16[4,2,256,128]{3,2,1,0:T(8,128)(2,1)S(1)} collective-permute-done((bf16[4,2,256,128]{3,2,1,0:T(8,128)(2,1)S(1)}, bf16[4,2,256,128]{3,2,1,0:T(8,128)(2,1)S(1)}, u32[]{:S(2)}, u32[]{:S(2)}) %collective-permute-start.58) | collective-permute-done | bytes 524320 | tf_op jit(solution)/shard_map/ppermute | solution.py:76
  309.3 11.6 %shard_map.175 = (f32[384,1024]{1,0:T(8,128)S(1)}, bf16[384,1024]{1,0:T(8,128)(2,1)S(1)}, bf16[2,2,256,128]{3,2,1,0:T(8,128)(2,1)S(1)}, bf16[2,2,256,128]{3,2,1,...) custom-call(s32[1]{0:T(128)} %bitcast.1.chip_ref, ...), custom_call_target="tpu_custom_call" | custom-call | flops 1837105152 | bytes 11534336 | tf_op jit(solution)/shard_map/pallas_call | solution.py:547
  329.0 3.7 all-to-all-start.3
  341.7 3.4 copy-done.1
  345.1 6.4 %shard_map.172 = bf16[16,256,1024]{2,1,0:T(8,128)(2,1)} custom-call(s32[16,1,32]{2,1,0:T(1,128)S(1)} %bitcast.73, bf16[16,256,1024]{2,1,0:T(8,128)(2,1)S(1)} %copy-done.1, bf16[16,32,1024]{2,1,0:T(8,128)(2,1)} %bitcast.24.rows_ref), custom_call_target="tpu_custom_call" | custom-call | flops 268435456 | bytes 16777216 | tf_op jit(solution)/shard_map/pallas_call | solution.py:267
  363.7 4.7 %shard_map.176 = bf16[16,256,1024]{2,1,0:T(8,128)(2,1)} custom-call(s32[16,1,32]{2,1,0:T(1,128)S(1)} %bitcast.74, bf16[16,256,1024]{2,1,0:T(8,128)(2,1)S(1)} %copy-done.3, bf16[16,32,1024]{2,1,0:T(8,128)(2,1)S(1)} %bitcast.72), custom_call_target="tpu_custom_call" | custom-call | flops 268435456 | bytes 16777216 | tf_op jit(solution)/shard_map/pallas_call | solution.py:267
  371.8 6.0 %collective-permute-done.79 = f32[3,1024]{1,0:T(4,128)S(1)} collective-permute-done((f32[3,1024]{1,0:T(4,128)S(1)}, f32[3,1024]{1,0:T(4,128)S(1)}, u32[]{:S(2)}, u32[]{:S(2)}) %collective-permute-start.79) | collective-permute-done | bytes 12320 | tf_op jit(solution)/shard_map/ppermute | solution.py:215
  387.2 3.9 collective-permute-done.82
  391.7 5.6 %shard_map.178 = f32[16384,128]{1,0:T(8,128)} custom-call(s32[1]{0:T(128)} %bitcast.1.chip_ref, s32[1]{0:T(128)} %bitcast.39.core_ref, bf16[2,128,1024]{2,1,0:T(8,128)(2,1)S(1)} %pad_maximum_fusion.17.refs_0_, bf16[2,128,1024]{2,1,0:T(8,128)(2,1)S(1)} %collective-permute-done.66.refs_1_, bf16[2,128,1024]{2,1,0:T(8,128)(2,1)S(1)} %pad_maximum_fusion.18.refs_2_, ...), custom_call_target="tpu_custom_call" | custom-call | bytes 12582912 | tf_op jit(solution)/shard_map/pallas_call | solution.py:728
  397.3 3.8 shard_map.177
  (567 shorter events, 197.3 us)
Async XLA Ops:
  13.6 21.1 %all-to-all-start = ((bf16[8,2,32,1024]{3,2,1,0:T(8,128)(2,1)}), bf16[8,2,32,1024]{3,2,1,0:T(8,128)(2,1)S(1)}, u32[]{:S(2)}, u32[]{:S(2)}) async-start(bf16[8,2,32,1024]{3,2,1,0:T(8,128)(2,1)} %bitcast.7), calls=%async_computation | async-start | bytes 2097152 | tf_op jit(solution)/shard_map/all_to_all | solution.py:824
  17.4 17.3 %collective-permute-start.3 = (bf16[1,4,256,128]{3,2,1,0:T(8,128)(2,1)S(1)}, bf16[1,4,256,128]{3,2,1,0:T(8,128)(2,1)S(1)}, u32[]{:S(2)}, u32[]{:S(2)}) collective-permute-start(bf16[1,4,256,128]{3,2,1,0:T(8,128)(2,1)S(1)} %collective-permute-done), channel_id=1, source_target_pairs={{0,1},{1,3},{3,2},{2,0},{4,5},{5,7},{7,6},{6,4},{8,9},{9,11},{11,1... | collective-permute-start | bytes 786440 | tf_op jit(solution)/shard_map/ppermute | solution.py:76
  55.4 17.6 %collective-permute-start.14 = (bf16[2,128,1024]{2,1,0:T(8,128)(2,1)S(1)}, bf16[2,128,1024]{2,1,0:T(8,128)(2,1)}, u32[]{:S(2)}, u32[]{:S(2)}) collective-permute-start(bf16[2,128,1024]{2,1,0:T(8,128)(2,1)S(1)} %pad_maximum_fusion.8), channel_id=1, source_target_pairs={{0,1},{1,3},{3,2},{2,0},{4,5},{5,7},{7,6},{6,4},{8,9},{9,11},{11,1... | collective-permute-start | bytes 1572872 | tf_op jit(solution)/shard_map/ppermute | solution.py:76
  73.0 20.8 %collective-permute-start.15 = (bf16[2,2,256,128]{3,2,1,0:T(8,128)(2,1)S(1)}, bf16[2,2,256,128]{3,2,1,0:T(8,128)(2,1)S(1)}, u32[]{:S(2)}, u32[]{:S(2)}) collective-permute-start(bf16[2,2,256,128]{3,2,1,0:T(8,128)(2,1)S(1)} %pad_maximum_fusion.23.refs_0_), channel_id=1, source_target_pairs={{0,16},{4,20},{8,24},{12,28},{16,0},{20,4},{24,8},{28,12},{1,17},{... | collective-permute-start | bytes 786440 | tf_op jit(solution)/shard_map/ppermute | solution.py:61
  74.6 19.3 %collective-permute-start.19 = (bf16[2,128,1024]{2,1,0:T(8,128)(2,1)}, bf16[2,128,1024]{2,1,0:T(8,128)(2,1)}, u32[]{:S(2)}, u32[]{:S(2)}) collective-permute-start(bf16[2,128,1024]{2,1,0:T(8,128)(2,1)} %collective-permute-done.14), channel_id=1, source_target_pairs={{0,1},{1,3},{3,2},{2,0},{4,5},{5,7},{7,6},{6,4},{8,9},{9,11},{11,1... | collective-permute-start | bytes 1572872 | tf_op jit(solution)/shard_map/ppermute | solution.py:76
  74.6 19.2 %collective-permute-start.16 = (bf16[2,2,256,128]{3,2,1,0:T(8,128)(2,1)S(1)}, bf16[2,2,256,128]{3,2,1,0:T(8,128)(2,1)S(1)}, u32[]{:S(2)}, u32[]{:S(2)}) collective-permute-start(bf16[2,2,256,128]{3,2,1,0:T(8,128)(2,1)S(1)} %pad_maximum_fusion.24.refs_2_), channel_id=1, source_target_pairs={{0,8},{4,12},{8,0},{12,4},{16,24},{20,28},{24,16},{28,20},{1,9},{5... | collective-permute-start | bytes 786440 | tf_op jit(solution)/shard_map/ppermute | solution.py:61
  79.2 37.7 %all-to-all-start.1 = ((bf16[8,2,32,1024]{3,2,1,0:T(8,128)(2,1)}), bf16[8,2,32,1024]{3,2,1,0:T(8,128)(2,1)}, u32[]{:S(2)}, u32[]{:S(2)}) async-start(bf16[8,2,32,1024]{3,2,1,0:T(8,128)(2,1)} %bitcast.12), calls=%async_computation.1 | async-start | bytes 2097152 | tf_op jit(solution)/shard_map/all_to_all | solution.py:824
  96.2 23.4 %collective-permute-start.20 = (bf16[2,128,1024]{2,1,0:T(8,128)(2,1)}, bf16[2,128,1024]{2,1,0:T(8,128)(2,1)}, u32[]{:S(2)}, u32[]{:S(2)}) collective-permute-start(bf16[2,128,1024]{2,1,0:T(8,128)(2,1)} %pad_maximum_fusion.9.refs_0_), channel_id=1, source_target_pairs={{0,16},{4,20},{8,24},{12,28},{16,0},{20,4},{24,8},{28,12},{1,17},{... | collective-permute-start | bytes 1572872 | tf_op jit(solution)/shard_map/ppermute | solution.py:61
  100.0 19.6 %collective-permute-start.21 = (bf16[2,128,1024]{2,1,0:T(8,128)(2,1)}, bf16[2,128,1024]{2,1,0:T(8,128)(2,1)}, u32[]{:S(2)}, u32[]{:S(2)}) collective-permute-start(bf16[2,128,1024]{2,1,0:T(8,128)(2,1)} %pad_maximum_fusion.10.refs_2_), channel_id=1, source_target_pairs={{0,8},{4,12},{8,0},{12,4},{16,24},{20,28},{24,16},{28,20},{1,9},{5... | collective-permute-start | bytes 1572872 | tf_op jit(solution)/shard_map/ppermute | solution.py:61
  101.5 18.2 %collective-permute-start.24 = (bf16[2,128,1024]{2,1,0:T(8,128)(2,1)}, bf16[2,128,1024]{2,1,0:T(8,128)(2,1)}, u32[]{:S(2)}, u32[]{:S(2)}) collective-permute-start(bf16[2,128,1024]{2,1,0:T(8,128)(2,1)} %collective-permute-done.19), channel_id=1, source_target_pairs={{0,1},{1,3},{3,2},{2,0},{4,5},{5,7},{7,6},{6,4},{8,9},{9,11},{11,1... | collective-permute-start | bytes 1572872 | tf_op jit(solution)/shard_map/ppermute | solution.py:76
  127.3 20.8 %collective-permute-start.28 = (bf16[2,128,1024]{2,1,0:T(8,128)(2,1)S(1)}, bf16[2,128,1024]{2,1,0:T(8,128)(2,1)S(1)}, u32[]{:S(2)}, u32[]{:S(2)}) collective-permute-start(bf16[2,128,1024]{2,1,0:T(8,128)(2,1)S(1)} %pad_maximum_fusion.11.refs_0_), channel_id=1, source_target_pairs={{0,16},{4,20},{8,24},{12,28},{16,0},{20,4},{24,8},{28,12},{1,17},{... | collective-permute-start | bytes 1572872 | tf_op jit(solution)/shard_map/ppermute | solution.py:61
  128.8 19.3 %collective-permute-start.29 = (bf16[2,128,1024]{2,1,0:T(8,128)(2,1)S(1)}, bf16[2,128,1024]{2,1,0:T(8,128)(2,1)S(1)}, u32[]{:S(2)}, u32[]{:S(2)}) collective-permute-start(bf16[2,128,1024]{2,1,0:T(8,128)(2,1)S(1)} %pad_maximum_fusion.12.refs_2_), channel_id=1, source_target_pairs={{0,8},{4,12},{8,0},{12,4},{16,24},{20,28},{24,16},{28,20},{1,9},{5... | collective-permute-start | bytes 1572872 | tf_op jit(solution)/shard_map/ppermute | solution.py:61
  151.5 22.2 %collective-permute-start.34 = (bf16[2,128,1024]{2,1,0:T(8,128)(2,1)S(1)}, bf16[2,128,1024]{2,1,0:T(8,128)(2,1)S(1)}, u32[]{:S(2)}, u32[]{:S(2)}) collective-permute-start(bf16[2,128,1024]{2,1,0:T(8,128)(2,1)S(1)} %get-tuple-element.288), channel_id=1, source_target_pairs={{0,8},{4,12},{8,0},{12,4},{16,24},{20,28},{24,16},{28,20},{1,9},{5... | collective-permute-start | bytes 1572872 | tf_op jit(solution)/shard_map/ppermute | solution.py:61
  152.1 21.6 %collective-permute-start.35 = (bf16[2,128,1024]{2,1,0:T(8,128)(2,1)S(1)}, bf16[2,128,1024]{2,1,0:T(8,128)(2,1)S(1)}, u32[]{:S(2)}, u32[]{:S(2)}) collective-permute-start(bf16[2,128,1024]{2,1,0:T(8,128)(2,1)S(1)} %get-tuple-element.289), channel_id=1, source_target_pairs={{0,16},{4,20},{8,24},{12,28},{16,0},{20,4},{24,8},{28,12},{1,17},{... | collective-permute-start | bytes 1572872 | tf_op jit(solution)/shard_map/ppermute | solution.py:61
  215.6 36.4 %all-to-all-start.2 = ((bf16[1,2,8,32,1024]{4,3,1,0,2:T(8,128)(2,1)}), bf16[1,2,8,32,1024]{4,3,1,0,2:T(8,128)(2,1)}, u32[]{:S(2)}, u32[]{:S(2)}) async-start(bf16[1,2,8,32,1024]{4,3,1,0,2:T(8,128)(2,1)} %pad_maximum_fusion.4), calls=%async_computation.2 | async-start | bytes 2097152 | tf_op jit(solution)/shard_map/all_to_all | solution.py:829
  220.1 31.2 %collective-permute-start.46 = (bf16[2,128,1024]{2,1,0:T(8,128)(2,1)S(1)}, bf16[2,128,1024]{2,1,0:T(8,128)(2,1)}, u32[]{:S(2)}, u32[]{:S(2)}) collective-permute-start(bf16[2,128,1024]{2,1,0:T(8,128)(2,1)S(1)} %pad_maximum_fusion.15), channel_id=1, source_target_pairs={{0,1},{1,3},{3,2},{2,0},{4,5},{5,7},{7,6},{6,4},{8,9},{9,11},{11,1... | collective-permute-start | bytes 1572872 | tf_op jit(solution)/shard_map/ppermute | solution.py:76
  221.9 23.1 %collective-permute-start.47 = (bf16[1,128,1024]{2,1,0:T(8,128)(2,1)S(1)}, bf16[1,128,1024]{2,1,0:T(8,128)(2,1)S(1)}, u32[]{:S(2)}, u32[]{:S(2)}) collective-permute-start(bf16[1,128,1024]{2,1,0:T(8,128)(2,1)S(1)} %add_convert_fusion.29), channel_id=1, source_target_pairs={{0,16},{4,20},{8,24},{12,28},{16,0},{20,4},{24,8},{28,12},{1,17},{... | collective-permute-start | bytes 786440 | tf_op jit(solution)/shard_map/ppermute | solution.py:61
  223.9 27.4 %collective-permute-start.49 = (bf16[2,128,1024]{2,1,0:T(8,128)(2,1)}, bf16[2,128,1024]{2,1,0:T(8,128)(2,1)}, u32[]{:S(2)}, u32[]{:S(2)}) collective-permute-start(bf16[2,128,1024]{2,1,0:T(8,128)(2,1)} %get-tuple-element.340), channel_id=1, source_target_pairs={{0,8},{4,12},{8,0},{12,4},{16,24},{20,28},{24,16},{28,20},{1,9},{5... | collective-permute-start | bytes 1572872 | tf_op jit(solution)/shard_map/ppermute | solution.py:61
  225.4 26.6 %collective-permute-start.50 = (bf16[2,128,1024]{2,1,0:T(8,128)(2,1)}, bf16[2,128,1024]{2,1,0:T(8,128)(2,1)}, u32[]{:S(2)}, u32[]{:S(2)}) collective-permute-start(bf16[2,128,1024]{2,1,0:T(8,128)(2,1)} %get-tuple-element.341), channel_id=1, source_target_pairs={{0,16},{4,20},{8,24},{12,28},{16,0},{20,4},{24,8},{28,12},{1,17},{... | collective-permute-start | bytes 1572872 | tf_op jit(solution)/shard_map/ppermute | solution.py:61
  226.1 25.2 %collective-permute-start.48 = (bf16[1,128,1024]{2,1,0:T(8,128)(2,1)S(1)}, bf16[1,128,1024]{2,1,0:T(8,128)(2,1)S(1)}, u32[]{:S(2)}, u32[]{:S(2)}) collective-permute-start(bf16[1,128,1024]{2,1,0:T(8,128)(2,1)S(1)} %add_convert_fusion.28), channel_id=1, source_target_pairs={{0,8},{4,12},{8,0},{12,4},{16,24},{20,28},{24,16},{28,20},{1,9},{5... | collective-permute-start | bytes 786440 | tf_op jit(solution)/shard_map/ppermute | solution.py:61
  256.1 20.5 %collective-permute-start.52 = (bf16[2,128,1024]{2,1,0:T(8,128)(2,1)S(1)}, bf16[2,128,1024]{2,1,0:T(8,128)(2,1)S(1)}, u32[]{:S(2)}, u32[]{:S(2)}) collective-permute-start(bf16[2,128,1024]{2,1,0:T(8,128)(2,1)S(1)} %add_convert_fusion.5), channel_id=1, source_target_pairs={{0,1},{1,3},{3,2},{2,0},{4,5},{5,7},{7,6},{6,4},{8,9},{9,11},{11,1... | collective-permute-start | bytes 1572872 | tf_op jit(solution)/shard_map/ppermute | solution.py:76
  258.0 18.6 %collective-permute-start.53 = (bf16[1,128,1024]{2,1,0:T(8,128)(2,1)S(1)}, bf16[1,128,1024]{2,1,0:T(8,128)(2,1)S(1)}, u32[]{:S(2)}, u32[]{:S(2)}) collective-permute-start(bf16[1,128,1024]{2,1,0:T(8,128)(2,1)S(1)} %add_convert_fusion.23), channel_id=1, source_target_pairs={{0,16},{4,20},{8,24},{12,28},{16,0},{20,4},{24,8},{28,12},{1,17},{... | collective-permute-start | bytes 786440 | tf_op jit(solution)/shard_map/ppermute | solution.py:61
  279.1 19.4 %collective-permute-start.57 = (bf16[2,128,1024]{2,1,0:T(8,128)(2,1)S(1)}, bf16[2,128,1024]{2,1,0:T(8,128)(2,1)S(1)}, u32[]{:S(2)}, u32[]{:S(2)}) collective-permute-start(bf16[2,128,1024]{2,1,0:T(8,128)(2,1)S(1)} %add_convert_fusion.4), channel_id=1, source_target_pairs={{0,1},{1,3},{3,2},{2,0},{4,5},{5,7},{7,6},{6,4},{8,9},{9,11},{11,1... | collective-permute-start | bytes 1572872 | tf_op jit(solution)/shard_map/ppermute | solution.py:76
  281.5 22.0 %collective-permute-start.58 = (bf16[4,2,256,128]{3,2,1,0:T(8,128)(2,1)S(1)}, bf16[4,2,256,128]{3,2,1,0:T(8,128)(2,1)S(1)}, u32[]{:S(2)}, u32[]{:S(2)}) collective-permute-start(bf16[4,2,256,128]{3,2,1,0:T(8,128)(2,1)S(1)} %pad_maximum_fusion.16), channel_id=1, source_target_pairs={{0,1},{1,3},{3,2},{2,0},{4,5},{5,7},{7,6},{6,4},{8,9},{9,11},{11,1... | collective-permute-start | bytes 1572872 | tf_op jit(solution)/shard_map/ppermute | solution.py:76
  321.3 33.1 %collective-permute-start.66 = (bf16[2,128,1024]{2,1,0:T(8,128)(2,1)S(1)}, bf16[2,128,1024]{2,1,0:T(8,128)(2,1)S(1)}, u32[]{:S(2)}, u32[]{:S(2)}) collective-permute-start(bf16[2,128,1024]{2,1,0:T(8,128)(2,1)S(1)} %pad_maximum_fusion.17.refs_0_), channel_id=1, source_target_pairs={{0,16},{4,20},{8,24},{12,28},{16,0},{20,4},{24,8},{28,12},{1,17},{... | collective-permute-start | bytes 1572872 | tf_op jit(solution)/shard_map/ppermute | solution.py:61
  322.8 31.6 %collective-permute-start.67 = (bf16[2,128,1024]{2,1,0:T(8,128)(2,1)S(1)}, bf16[2,128,1024]{2,1,0:T(8,128)(2,1)S(1)}, u32[]{:S(2)}, u32[]{:S(2)}) collective-permute-start(bf16[2,128,1024]{2,1,0:T(8,128)(2,1)S(1)} %pad_maximum_fusion.18.refs_2_), channel_id=1, source_target_pairs={{0,8},{4,12},{8,0},{12,4},{16,24},{20,28},{24,16},{28,20},{1,9},{5... | collective-permute-start | bytes 1572872 | tf_op jit(solution)/shard_map/ppermute | solution.py:61
  329.0 25.6 %all-to-all-start.3 = ((bf16[1,2,8,32,1024]{4,3,1,0,2:T(8,128)(2,1)}), bf16[1,2,8,32,1024]{4,3,1,0,2:T(8,128)(2,1)S(1)}, u32[]{:S(2)}, u32[]{:S(2)}) async-start(bf16[1,2,8,32,1024]{4,3,1,0,2:T(8,128)(2,1)} %pad_maximum_fusion.5), calls=%async_computation.3 | async-start | bytes 2097152 | tf_op jit(solution)/shard_map/all_to_all | solution.py:829
  335.1 19.5 %collective-permute-start.68 = (bf16[4,2,256,128]{3,2,1,0:T(8,128)(2,1)S(1)}, bf16[4,2,256,128]{3,2,1,0:T(8,128)(2,1)}, u32[]{:S(2)}, u32[]{:S(2)}) collective-permute-start(bf16[4,2,256,128]{3,2,1,0:T(8,128)(2,1)S(1)} %add_convert_fusion.1), channel_id=1, source_target_pairs={{0,1},{1,3},{3,2},{2,0},{4,5},{5,7},{7,6},{6,4},{8,9},{9,11},{11,1... | collective-permute-start | bytes 1572872 | tf_op jit(solution)/shard_map/ppermute | solution.py:76
  378.8 18.4 %collective-permute-start.85 = (bf16[2,2,256,128]{3,2,1,0:T(8,128)(2,1)S(1)}, bf16[2,2,256,128]{3,2,1,0:T(8,128)(2,1)S(1)}, u32[]{:S(2)}, u32[]{:S(2)}) collective-permute-start(bf16[2,2,256,128]{3,2,1,0:T(8,128)(2,1)S(1)} %get-tuple-element.451.refs_0_), channel_id=1, source_target_pairs={{0,4},{4,0},{8,12},{12,8},{16,20},{20,16},{24,28},{28,24},{1,5},{5... | collective-permute-start | bytes 786440 | tf_op jit(solution)/shard_map/ppermute | solution.py:61
  378.8 18.4 %collective-permute-start.87 = (bf16[2,2,256,128]{3,2,1,0:T(8,128)(2,1)S(1)}, bf16[2,2,256,128]{3,2,1,0:T(8,128)(2,1)S(1)}, u32[]{:S(2)}, u32[]{:S(2)}) collective-permute-start(bf16[2,2,256,128]{3,2,1,0:T(8,128)(2,1)S(1)} %get-tuple-element.450.refs_2_), channel_id=1, source_target_pairs={{0,4},{4,0},{8,12},{12,8},{16,20},{20,16},{24,28},{28,24},{1,5},{5... | collective-permute-start | bytes 786440 | tf_op jit(solution)/shard_map/ppermute | solution.py:61
  379.3 17.9 %collective-permute-start.86 = (bf16[2,2,256,128]{3,2,1,0:T(8,128)(2,1)S(1)}, bf16[2,2,256,128]{3,2,1,0:T(8,128)(2,1)S(1)}, u32[]{:S(2)}, u32[]{:S(2)}) collective-permute-start(bf16[2,2,256,128]{3,2,1,0:T(8,128)(2,1)S(1)} %collective-permute-done.83.refs_1_), channel_id=1, source_target_pairs={{0,4},{4,0},{8,12},{12,8},{16,20},{20,16},{24,28},{28,24},{1,5},{5... | collective-permute-start | bytes 786440 | tf_op jit(solution)/shard_map/ppermute | solution.py:61
  379.3 17.9 %collective-permute-start.88 = (bf16[2,2,256,128]{3,2,1,0:T(8,128)(2,1)S(1)}, bf16[2,2,256,128]{3,2,1,0:T(8,128)(2,1)S(1)}, u32[]{:S(2)}, u32[]{:S(2)}) collective-permute-start(bf16[2,2,256,128]{3,2,1,0:T(8,128)(2,1)S(1)} %collective-permute-done.84.refs_3_), channel_id=1, source_target_pairs={{0,4},{4,0},{8,12},{12,8},{16,20},{20,16},{24,28},{28,24},{1,5},{5... | collective-permute-start | bytes 786440 | tf_op jit(solution)/shard_map/ppermute | solution.py:61
  (205 other events, 1569.2 us)
